TPU v7x, 1024 devices: a whole 4x8x16 slice. The times are simulated.
1024 devices in a mesh: grp: 16 (over z), dev: 64 (over y, x, core).
Axes of the slice: x: 4, y: 8, z: 16, core: 2. Of those that a mesh axis runs over, the one named last changes fastest.
Arguments:
- fields: float32 [4096, 6, 16, 256], P(('grp', 'dev')), may hold values from 0 to 1
- swap_dev: int32 [1024], P(('grp', 'dev')), may hold values from 0 to 1, as said below
- swap_grp: int32 [1024], P(('grp', 'dev')), may hold values from 0 to 1, as said below
- neighbors: int32 [4096, 6], P(('grp', 'dev')), may hold values from -1 to 4095, as said below
- orient: int32 [4096], P(('grp', 'dev')), may hold values from 0 to 7
Outputs:
- advanced: float32 [4096, 6, 16, 256], P(('grp', 'dev'))
Inputs may be any that keep to these rules, and one draw needn't show every extreme that they name: `swap_dev`: equal on devices 2i and 2i+1 of each group. `swap_grp`: equal on the devices of one dev index in groups 2j and 2j+1. `neighbors`: adjacency is mutual: b names n across a face exactly when n names b across the opposite face. Neighbours across -x and -y lie on the same device or the previous dev index of the same group, across +x and +y on the same device or the next dev index of the same group; across -z and +z on the same dev index of the previous and the next group.
All inputs are finite; a program needn't handle non-finite values.
Results may differ from a plain program's by a relative error of at most 0.0001.
Values sent between devices are 32-bit elements; how exact they have to be, the bound alone decides.
A program may use at most 32 MiB of HBM per device.

v0:
```python
import math

import jax
import jax.numpy as jnp
from jax import lax
from jax.sharding import PartitionSpec as P

NPHASE = 4
NCONC = 2
NORI = 8
STEPS = 2


phase_rate = 0.05
closure = 0.1
coupling = (0.5, -0.5, 1.0, -1.0)
conc_rates = (0.08, 0.04)


def padded(block, sides, width):
    for axis, dim in sides:
        count = lax.axis_size(axis)
        forward = [(i, i + 1) for i in range(count - 1)]
        backward = [(target, source) for source, target in forward]
        low = lax.ppermute(
            lax.slice_in_dim(block, block.shape[dim] - width, None, axis=dim), axis, forward
        )
        high = lax.ppermute(lax.slice_in_dim(block, 0, width, axis=dim), axis, backward)
        block = jnp.concatenate([low, block, high], axis=dim)
    return block


def swapped(block, axis, bit):
    count = lax.axis_size(axis)
    route = []
    for low in range(count):
        high = low | 1 << bit
        if high != low and high < count:
            route += [(low, high), (high, low)]
    return lax.ppermute(block, axis, route)


def coefficients(orient):
    theta = math.pi * orient.astype(jnp.float32) / NORI
    return (
        1.0 + 0.5 * jnp.cos(2.0 * theta),
        1.0 - 0.5 * jnp.cos(2.0 * theta),
        1.0 + 0.5 * jnp.sin(2.0 * theta),
    )


def face_table(state, edge, plane):
    slots, nfield = (state.shape[0], state.shape[1])
    lower_x = state[:, :, 0]
    upper_x = state[:, :, edge - 1]
    lower_y = state[:, :, :, 0:edge].reshape(slots, nfield, plane)
    upper_y = state[:, :, :, plane - edge :].reshape(slots, nfield, plane)
    lower_z = state[:, :, :, 0::edge].reshape(slots, nfield, plane)
    upper_z = state[:, :, :, edge - 1 :: edge].reshape(slots, nfield, plane)
    return jnp.stack([lower_x, upper_x, lower_y, upper_y, lower_z, upper_z], axis=1)


def one_step(state, neighbors, rank, scales):
    slots, nfield, edge, plane = state.shape
    table = face_table(state, edge, plane)
    beside = padded(table[:, 0:4][None], (("dev", 0),), 1)
    across = padded(table[:, 4:6][None], (("grp", 0),), 1)
    remote_tables = [
        beside[0][:, 1],
        beside[2][:, 0],
        beside[0][:, 3],
        beside[2][:, 2],
        across[0][:, 1],
        across[2][:, 0],
    ]
    ghosts = []
    for face in range(6):
        opposite = face + 1 - 2 * (face % 2)
        target = neighbors[:, face]
        slot_index = jnp.remainder(target, slots)
        owner = jnp.floor_divide(target, slots)
        local = jnp.take(table[:, opposite], slot_index, axis=0)
        remote = jnp.take(remote_tables[face], slot_index, axis=0)
        picked = jnp.where((owner == rank).reshape(-1, 1, 1), local, remote)
        ghosts.append(jnp.where((target < 0).reshape(-1, 1, 1), table[:, face], picked))
    padded_x = jnp.concatenate([ghosts[0][:, :, None], state, ghosts[1][:, :, None]], axis=2)
    sum_x = padded_x[:, :, 2:] + padded_x[:, :, :-2]
    wall_low_y = ghosts[2].reshape(slots, nfield, edge, edge)
    wall_high_y = ghosts[3].reshape(slots, nfield, edge, edge)
    padded_y = jnp.concatenate([wall_low_y, state, wall_high_y], axis=3)
    sum_y = padded_y[..., 2 * edge :] + padded_y[..., :plane]
    wall_low_z = jnp.broadcast_to(
        ghosts[4].reshape(slots, nfield, edge, edge, 1), (slots, nfield, edge, edge, edge)
    ).reshape(slots, nfield, edge, plane)
    wall_high_z = jnp.broadcast_to(
        ghosts[5].reshape(slots, nfield, edge, edge, 1), (slots, nfield, edge, edge, edge)
    ).reshape(slots, nfield, edge, plane)
    position = jnp.arange(plane) % edge
    zeros_column = jnp.zeros((slots, nfield, edge, 1), state.dtype)
    below = jnp.concatenate([zeros_column, state[..., :-1]], axis=3)
    below = jnp.where(position == 0, wall_low_z, below)
    above = jnp.concatenate([state[..., 1:], zeros_column], axis=3)
    above = jnp.where(position == edge - 1, wall_high_z, above)
    sum_z = above + below
    weight_x, weight_y, weight_z = scales
    aniso = (
        weight_x * (sum_x - 2.0 * state)
        + weight_y * (sum_y - 2.0 * state)
        + weight_z * (sum_z - 2.0 * state)
    )
    iso = sum_x + sum_y + sum_z - 6.0 * state
    phases = state[:, :NPHASE]
    conc = state[:, NPHASE:]
    total = jnp.sum(phases, axis=1, keepdims=True)
    drive = conc[:, 0:1] - conc[:, 1:2]
    beta = jnp.array(coupling, jnp.float32).reshape(1, NPHASE, 1, 1)
    rates = jnp.array(conc_rates, jnp.float32).reshape(1, NCONC, 1, 1)
    well = phases * (1.0 - phases) * (1.0 - 2.0 * phases)
    new_phases = phases + phase_rate * (
        aniso[:, :NPHASE] - well + beta * drive * phases * (1.0 - phases) - closure * (total - 1.0)
    )
    new_conc = conc + rates * iso[:, NPHASE:]
    return jnp.concatenate([new_phases, new_conc], axis=1)


def body(fields, swap_dev, swap_grp, neighbors, orient):
    slots = fields.shape[0]
    last_block = fields[slots - 1]
    arrived = swapped(last_block, "dev", 0)
    fields = fields.at[slots - 1].set(jnp.where(swap_dev[0] == 1, arrived, last_block))
    first_block = fields[0]
    arrived = swapped(first_block, "grp", 0)
    fields = fields.at[0].set(jnp.where(swap_grp[0] == 1, arrived, first_block))
    rank = lax.axis_index("grp") * lax.axis_size("dev") + lax.axis_index("dev")
    weight_x, weight_y, weight_z = coefficients(orient)
    scales = (
        weight_x.reshape(-1, 1, 1, 1),
        weight_y.reshape(-1, 1, 1, 1),
        weight_z.reshape(-1, 1, 1, 1),
    )
    state = fields
    for step in range(STEPS):
        state = one_step(state, neighbors, rank, scales)
    return state


def solution(mesh):
    in_specs = (
        P(("grp", "dev"), None, None, None),
        P(("grp", "dev")),
        P(("grp", "dev")),
        P(("grp", "dev"), None),
        P(("grp", "dev")),
    )
    out_specs = P(("grp", "dev"), None, None, None)
    return jax.shard_map(body, mesh=mesh, in_specs=in_specs, out_specs=out_specs, check_vma=False)
```

profile of v0, /device:TPU:1, one launch (start us, length us, event | category | flops | bytes accessed | tf_op | source)
XLA Modules:
  0.0 118.6 jit_solution(9651870871187075917)
XLA Ops:
  0.0 0.9 slice.236
  1.0 16.1 %collective-permute-start = (f32[6,16,256]{2,0,1:T(8,128)S(1)}, f32[6,16,256]{2,0,1:T(8,128)S(1)}, u32[]{:S(2)}, u32[]{:S(2)}) collective-permute-start(f32[6,16,256]{2,0,1:T(8,128)S(1)} %bitcast.165), channel_id=1, source_target_pairs={{0,1},{1,0},{2,3},{3,2},{4,5},{5,4},{6,7},{7,6},{8,9},{9,8},{10,11... | collective-permute-start | bytes 294920 | tf_op jit(solution)/shard_map/ppermute | solution.py:40
  17.0 1.2 %copy.109 = f32[4,6,16,256]{3,1,0,2:T(8,128)S(1)} copy(f32[4,6,16,256]{3,2,1,0:T(8,128)} %param.15) | data formatting | bytes 786432 | tf_op args[0]
  19.6 1.2 slice_reduce_fusion.6
  25.0 1.3 %broadcast_add_fusion = (f32[4]{0:T(128)}, f32[4]{0:T(128)}, f32[4]{0:T(128)}) fusion(s32[4]{0:T(128)} %param.19), kind=kLoop, calls=%fused_computation.248 | loop fusion | flops 28 | bytes 64 | tf_op jit(solution)/shard_map/add | solution.py:46
  26.9 1.9 %collective-permute-start.1 = (f32[6,16,256]{2,0,1:T(8,128)S(1)}, f32[6,16,256]{2,0,1:T(8,128)S(1)}, u32[]{:S(2)}, u32[]{:S(2)}) collective-permute-start(f32[6,16,256]{2,0,1:T(8,128)S(1)} %slice_bitcast_fusion), channel_id=1, source_target_pairs={{0,64},{64,0},{128,192},{192,128},{256,320},{320,256},{384,448},{4... | collective-permute-start | bytes 294920 | tf_op jit(solution)/shard_map/ppermute | solution.py:40
  29.4 4.5 %collective-permute-done.1 = f32[6,16,256]{2,0,1:T(8,128)S(1)} collective-permute-done((f32[6,16,256]{2,0,1:T(8,128)S(1)}, f32[6,16,256]{2,0,1:T(8,128)S(1)}, u32[]{:S(2)}, u32[]{:S(2)}) %collective-permute-start.1) | collective-permute-done | bytes 98336 | tf_op jit(solution)/shard_map/ppermute | solution.py:40
  33.9 2.2 %slice.256 = f32[4,6,16,16]{3,1,0,2:T(8,128)S(1)} slice(f32[4,6,16,256]{3,1,0,2:T(8,128)S(1)} %bitcast_dynamic-update-slice_fusion), slice={[0:4:1], [0:6:1], [0:16:1], [15:256:16]} | slice | bytes 49152 | tf_op jit(solution)/shard_map/slice | solution.py:59
  36.2 2.2 %slice.257 = f32[4,6,16,16]{3,1,0,2:T(8,128)S(1)} slice(f32[4,6,16,256]{3,1,0,2:T(8,128)S(1)} %bitcast_dynamic-update-slice_fusion), slice={[0:4:1], [0:6:1], [0:16:1], [0:256:16]} | slice | bytes 49152 | tf_op jit(solution)/shard_map/slice | solution.py:58
  39.0 2.7 %collective-permute-start.5 = (f32[1,4,2,6,256]{4,3,1,2,0:T(8,128)S(1)}, f32[1,4,2,6,256]{4,3,1,2,0:T(8,128)}, u32[]{:S(2)}, u32[]{:S(2)}) collective-permute-start(f32[1,4,2,6,256]{4,3,1,2,0:T(8,128)S(1)} %maximum_bitcast_fusion.2), channel_id=1, source_target_pairs={{0,64},{64,128},{128,192},{192,256},{256,320},{320,384},{384,448},... | collective-permute-start | bytes 147464 | tf_op jit(solution)/shard_map/ppermute | solution.py:25
  41.7 1.3 %collective-permute-start.4 = (f32[1,4,2,6,256]{4,3,1,2,0:T(8,128)S(1)}, f32[1,4,2,6,256]{4,3,1,2,0:T(8,128)S(1)}, u32[]{:S(2)}, u32[]{:S(2)}) collective-permute-start(f32[1,4,2,6,256]{4,3,1,2,0:T(8,128)S(1)} %maximum_bitcast_fusion.2), channel_id=1, source_target_pairs={{64,0},{128,64},{192,128},{256,192},{320,256},{384,320},{448,384},... | collective-permute-start | bytes 147464 | tf_op jit(solution)/shard_map/ppermute | solution.py:28
  43.9 2.8 %collective-permute-start.2 = (f32[1,4,4,6,256]{4,3,1,2,0:T(8,128)S(1)}, f32[1,4,4,6,256]{4,3,1,2,0:T(8,128)S(1)}, u32[]{:S(2)}, u32[]{:S(2)}) collective-permute-start(f32[1,4,4,6,256]{4,3,1,2,0:T(8,128)S(1)} %maximum_bitcast_fusion), channel_id=1, source_target_pairs={{1,0},{2,1},{3,2},{4,3},{5,4},{6,5},{7,6},{8,7},{9,8},{10,9},{11,1... | collective-permute-start | bytes 294920 | tf_op jit(solution)/shard_map/ppermute | solution.py:28
  46.7 2.8 %collective-permute-start.3 = (f32[1,4,4,6,256]{4,3,1,2,0:T(8,128)S(1)}, f32[1,4,4,6,256]{4,3,1,2,0:T(8,128)S(1)}, u32[]{:S(2)}, u32[]{:S(2)}) collective-permute-start(f32[1,4,4,6,256]{4,3,1,2,0:T(8,128)S(1)} %maximum_bitcast_fusion), channel_id=1, source_target_pairs={{0,1},{1,2},{2,3},{3,4},{4,5},{5,6},{6,7},{7,8},{8,9},{9,10},{10,1... | collective-permute-start | bytes 294920 | tf_op jit(solution)/shard_map/ppermute | solution.py:25
  51.5 0.7 gather_fusion.2
  52.2 0.7 gather_fusion.4
  52.9 0.8 slice_bitcast_fusion.7
  54.3 0.7 gather_fusion.11
  55.0 0.8 fusion.51
  55.8 0.7 gather_fusion.10
  56.5 0.7 fusion.50
  57.3 2.1 %broadcast_in_dim.196 = f32[4,6,16,16,16]{4,3,2,1,0:T(8,128)} broadcast(f32[4,6,16,16]{3,2,1,0:T(8,128)S(1)} %reshape.632), dimensions={0,1,2,3} | broadcast | bytes 417792 | tf_op jit(solution)/shard_map/broadcast_in_dim | solution.py:92
  59.4 2.8 %reshape.360 = f32[4,6,16,256]{3,2,1,0:T(8,128)S(1)} reshape(f32[4,6,16,16,16]{4,3,2,1,0:T(8,128)} %broadcast_in_dim.196) | data formatting | bytes 786432 | tf_op jit(solution)/shard_map/reshape | solution.py:94
  62.3 2.1 %broadcast_in_dim.191 = f32[4,6,16,16,16]{4,3,2,1,0:T(8,128)} broadcast(f32[4,6,16,16]{3,2,1,0:T(8,128)S(1)} %reshape.631), dimensions={0,1,2,3} | broadcast | bytes 417792 | tf_op jit(solution)/shard_map/broadcast_in_dim | solution.py:95
  64.5 2.8 %reshape.359 = f32[4,6,16,256]{3,2,1,0:T(8,128)S(1)} reshape(f32[4,6,16,16,16]{4,3,2,1,0:T(8,128)} %broadcast_in_dim.191) | data formatting | bytes 786432 | tf_op jit(solution)/shard_map/reshape | solution.py:97
  67.3 1.2 fusion.7
  71.3 0.7 fusion.53
  72.0 0.7 gather_fusion.6
  72.7 0.8 fusion.52
  73.9 0.8 fusion.57
  77.0 1.9 %collective-permute-start.7 = (f32[1,4,4,6,256]{4,3,1,2,0:T(8,128)S(1)}, f32[1,4,4,6,256]{4,3,1,2,0:T(8,128)S(1)}, u32[]{:S(2)}, u32[]{:S(2)}) collective-permute-start(f32[1,4,4,6,256]{4,3,1,2,0:T(8,128)S(1)} %maximum_bitcast_fusion.1), channel_id=1, source_target_pairs={{0,1},{1,2},{2,3},{3,4},{4,5},{5,6},{6,7},{7,8},{8,9},{9,10},{10,1... | collective-permute-start | bytes 294920 | tf_op jit(solution)/shard_map/ppermute | solution.py:25
  78.9 2.6 %collective-permute-start.6 = (f32[1,4,4,6,256]{4,3,1,2,0:T(8,128)S(1)}, f32[1,4,4,6,256]{4,3,1,2,0:T(8,128)S(1)}, u32[]{:S(2)}, u32[]{:S(2)}) collective-permute-start(f32[1,4,4,6,256]{4,3,1,2,0:T(8,128)S(1)} %maximum_bitcast_fusion.1), channel_id=1, source_target_pairs={{1,0},{2,1},{3,2},{4,3},{5,4},{6,5},{7,6},{8,7},{9,8},{10,9},{11,1... | collective-permute-start | bytes 294920 | tf_op jit(solution)/shard_map/ppermute | solution.py:28
  83.2 0.7 gather_fusion.16
  85.9 0.7 gather_fusion.19
  86.5 0.7 gather_fusion.17
  88.8 0.8 fusion.3
  89.6 2.2 %slice.280 = f32[4,6,16,16]{3,1,0,2:T(8,128)S(1)} slice(f32[4,6,16,256]{3,1,0,2:T(8,128)S(1)} %get-tuple-element.64), slice={[0:4:1], [0:6:1], [0:16:1], [15:256:16]} | slice | bytes 49152 | tf_op jit(solution)/shard_map/slice | solution.py:59
  91.8 2.2 %slice.281 = f32[4,6,16,16]{3,1,0,2:T(8,128)S(1)} slice(f32[4,6,16,256]{3,1,0,2:T(8,128)S(1)} %get-tuple-element.64), slice={[0:4:1], [0:6:1], [0:16:1], [0:256:16]} | slice | bytes 49152 | tf_op jit(solution)/shard_map/slice | solution.py:58
  94.6 4.0 %collective-permute-start.9 = (f32[1,4,2,6,256]{4,3,1,2,0:T(8,128)S(1)}, f32[1,4,2,6,256]{4,3,1,2,0:T(8,128)S(1)}, u32[]{:S(2)}, u32[]{:S(2)}) collective-permute-start(f32[1,4,2,6,256]{4,3,1,2,0:T(8,128)S(1)} %maximum_bitcast_fusion.3), channel_id=1, source_target_pairs={{0,64},{64,128},{128,192},{192,256},{256,320},{320,384},{384,448},... | collective-permute-start | bytes 147464 | tf_op jit(solution)/shard_map/ppermute | solution.py:25
  99.0 1.3 %collective-permute-start.8 = (f32[1,4,2,6,256]{4,3,1,2,0:T(8,128)S(1)}, f32[1,4,2,6,256]{4,3,1,2,0:T(8,128)S(1)}, u32[]{:S(2)}, u32[]{:S(2)}) collective-permute-start(f32[1,4,2,6,256]{4,3,1,2,0:T(8,128)S(1)} %maximum_bitcast_fusion.3), channel_id=1, source_target_pairs={{64,0},{128,64},{192,128},{256,192},{320,256},{384,320},{448,384},... | collective-permute-start | bytes 147464 | tf_op jit(solution)/shard_map/ppermute | solution.py:28
  100.6 0.7 gather_fusion.20
  101.3 0.7 gather_fusion.23
  101.9 2.3 %collective-permute-done.8 = f32[1,4,2,6,256]{4,3,1,2,0:T(8,128)S(1)} collective-permute-done((f32[1,4,2,6,256]{4,3,1,2,0:T(8,128)S(1)}, f32[1,4,2,6,256]{4,3,1,2,0:T(8,128)S(1)}, u32[]{:S(2)}, u32[]{:S(2)}) %collective-permute-start.8) | collective-permute-done | bytes 49184 | tf_op jit(solution)/shard_map/ppermute | solution.py:28
  105.1 0.7 gather_fusion.22
  106.0 2.1 %broadcast_in_dim.204 = f32[4,6,16,16,16]{4,3,2,1,0:T(8,128)} broadcast(f32[4,6,16,16]{3,2,1,0:T(8,128)S(1)} %reshape.636), dimensions={0,1,2,3} | broadcast | bytes 417792 | tf_op jit(solution)/shard_map/broadcast_in_dim | solution.py:92
  108.1 2.8 %reshape.364 = f32[4,6,16,256]{3,2,1,0:T(8,128)S(1)} reshape(f32[4,6,16,16,16]{4,3,2,1,0:T(8,128)} %broadcast_in_dim.204) | data formatting | bytes 786432 | tf_op jit(solution)/shard_map/reshape | solution.py:94
  111.1 2.1 %broadcast_in_dim.202 = f32[4,6,16,16,16]{4,3,2,1,0:T(8,128)} broadcast(f32[4,6,16,16]{3,2,1,0:T(8,128)S(1)} %reshape.635), dimensions={0,1,2,3} | broadcast | bytes 417792 | tf_op jit(solution)/shard_map/broadcast_in_dim | solution.py:95
  113.2 2.8 %reshape.363 = f32[4,6,16,256]{3,2,1,0:T(8,128)S(1)} reshape(f32[4,6,16,16,16]{4,3,2,1,0:T(8,128)} %broadcast_in_dim.202) | data formatting | bytes 786432 | tf_op jit(solution)/shard_map/reshape | solution.py:97
  117.6 1.0 copy.174
  (185 shorter events, 23.7 us)
Async XLA Ops:
  1.0 25.9 %collective-permute-start = (f32[6,16,256]{2,0,1:T(8,128)S(1)}, f32[6,16,256]{2,0,1:T(8,128)S(1)}, u32[]{:S(2)}, u32[]{:S(2)}) collective-permute-start(f32[6,16,256]{2,0,1:T(8,128)S(1)} %bitcast.165), channel_id=1, source_target_pairs={{0,1},{1,0},{2,3},{3,2},{4,5},{5,4},{6,7},{7,6},{8,9},{9,8},{10,11... | collective-permute-start | bytes 294920 | tf_op jit(solution)/shard_map/ppermute | solution.py:40
  22.5 27.9 %copy-start = (s32[1024]{0:T(1024)}, s32[1024]{0:T(1024)S(1)}, u32[]{:S(2)}) copy-start(s32[1024]{0:T(1024)S(1)} %pad_clamp_fusion.1) | copy-start | bytes 12292
  23.1 27.8 %copy-start.1 = (s32[1024]{0:T(1024)}, s32[1024]{0:T(1024)S(1)}, u32[]{:S(2)}) copy-start(s32[1024]{0:T(1024)S(1)} %pad_clamp_fusion.5) | copy-start | bytes 12292
  26.9 7.0 %collective-permute-start.1 = (f32[6,16,256]{2,0,1:T(8,128)S(1)}, f32[6,16,256]{2,0,1:T(8,128)S(1)}, u32[]{:S(2)}, u32[]{:S(2)}) collective-permute-start(f32[6,16,256]{2,0,1:T(8,128)S(1)} %slice_bitcast_fusion), channel_id=1, source_target_pairs={{0,64},{64,0},{128,192},{192,128},{256,320},{320,256},{384,448},{4... | collective-permute-start | bytes 294920 | tf_op jit(solution)/shard_map/ppermute | solution.py:40
  39.0 13.9 %collective-permute-start.5 = (f32[1,4,2,6,256]{4,3,1,2,0:T(8,128)S(1)}, f32[1,4,2,6,256]{4,3,1,2,0:T(8,128)}, u32[]{:S(2)}, u32[]{:S(2)}) collective-permute-start(f32[1,4,2,6,256]{4,3,1,2,0:T(8,128)S(1)} %maximum_bitcast_fusion.2), channel_id=1, source_target_pairs={{0,64},{64,128},{128,192},{192,256},{256,320},{320,384},{384,448},... | collective-permute-start | bytes 147464 | tf_op jit(solution)/shard_map/ppermute | solution.py:25
  41.7 12.0 %collective-permute-start.4 = (f32[1,4,2,6,256]{4,3,1,2,0:T(8,128)S(1)}, f32[1,4,2,6,256]{4,3,1,2,0:T(8,128)S(1)}, u32[]{:S(2)}, u32[]{:S(2)}) collective-permute-start(f32[1,4,2,6,256]{4,3,1,2,0:T(8,128)S(1)} %maximum_bitcast_fusion.2), channel_id=1, source_target_pairs={{64,0},{128,64},{192,128},{256,192},{320,256},{384,320},{448,384},... | collective-permute-start | bytes 147464 | tf_op jit(solution)/shard_map/ppermute | solution.py:28
  43.9 24.6 %collective-permute-start.2 = (f32[1,4,4,6,256]{4,3,1,2,0:T(8,128)S(1)}, f32[1,4,4,6,256]{4,3,1,2,0:T(8,128)S(1)}, u32[]{:S(2)}, u32[]{:S(2)}) collective-permute-start(f32[1,4,4,6,256]{4,3,1,2,0:T(8,128)S(1)} %maximum_bitcast_fusion), channel_id=1, source_target_pairs={{1,0},{2,1},{3,2},{4,3},{5,4},{6,5},{7,6},{8,7},{9,8},{10,9},{11,1... | collective-permute-start | bytes 294920 | tf_op jit(solution)/shard_map/ppermute | solution.py:28
  46.7 22.5 %collective-permute-start.3 = (f32[1,4,4,6,256]{4,3,1,2,0:T(8,128)S(1)}, f32[1,4,4,6,256]{4,3,1,2,0:T(8,128)S(1)}, u32[]{:S(2)}, u32[]{:S(2)}) collective-permute-start(f32[1,4,4,6,256]{4,3,1,2,0:T(8,128)S(1)} %maximum_bitcast_fusion), channel_id=1, source_target_pairs={{0,1},{1,2},{2,3},{3,4},{4,5},{5,6},{6,7},{7,8},{8,9},{9,10},{10,1... | collective-permute-start | bytes 294920 | tf_op jit(solution)/shard_map/ppermute | solution.py:25
  68.5 6.6 %copy-start.28 = (f32[2]{0:T(128)S(1)}, f32[2]{0:T(128)}, u32[]{:S(2)}) copy-start(f32[2]{0:T(128)} %constant.250.clone) | copy-start | bytes 28
  68.5 6.9 %copy-start.5 = (f32[4]{0:T(128)S(1)}, f32[4]{0:T(128)}, u32[]{:S(2)}) copy-start(f32[4]{0:T(128)} %get-tuple-element.87) | copy-start | bytes 52
  68.5 6.9 %copy-start.7 = (f32[4]{0:T(128)S(1)}, f32[4]{0:T(128)}, u32[]{:S(2)}) copy-start(f32[4]{0:T(128)} %get-tuple-element.88) | copy-start | bytes 52
  68.5 6.9 %copy-start.9 = (f32[4]{0:T(128)S(1)}, f32[4]{0:T(128)}, u32[]{:S(2)}) copy-start(f32[4]{0:T(128)} %get-tuple-element.89) | copy-start | bytes 52
  68.5 6.9 %copy-start.26 = (f32[4]{0:T(128)S(1)}, f32[4]{0:T(128)}, u32[]{:S(2)}) copy-start(f32[4]{0:T(128)} %constant.249.clone) | copy-start | bytes 52
  75.4 11.8 %copy-start.23 = (pred[4]{0:T(512)(128)(4,1)S(1)}, pred[4]{0:T(512)(128)(4,1)}, u32[]{:S(2)}) copy-start(pred[4]{0:T(512)(128)(4,1)} %get-tuple-element.102) | copy-start | bytes 16
  75.4 11.8 %copy-start.24 = (pred[4]{0:T(512)(128)(4,1)S(1)}, pred[4]{0:T(512)(128)(4,1)}, u32[]{:S(2)}) copy-start(pred[4]{0:T(512)(128)(4,1)} %get-tuple-element.103) | copy-start | bytes 16
  75.4 11.8 %copy-start.25 = (pred[4]{0:T(512)(128)(4,1)S(1)}, pred[4]{0:T(512)(128)(4,1)}, u32[]{:S(2)}) copy-start(pred[4]{0:T(512)(128)(4,1)} %get-tuple-element.104) | copy-start | bytes 16
  75.5 12.6 %copy-start.20 = (pred[4]{0:T(512)(128)(4,1)S(1)}, pred[4]{0:T(512)(128)(4,1)}, u32[]{:S(2)}) copy-start(pred[4]{0:T(512)(128)(4,1)} %get-tuple-element.44) | copy-start | bytes 16
  75.5 12.6 %copy-start.21 = (pred[4]{0:T(512)(128)(4,1)S(1)}, pred[4]{0:T(512)(128)(4,1)}, u32[]{:S(2)}) copy-start(pred[4]{0:T(512)(128)(4,1)} %get-tuple-element.96) | copy-start | bytes 16
  75.5 12.6 %copy-start.22 = (pred[4]{0:T(512)(128)(4,1)S(1)}, pred[4]{0:T(512)(128)(4,1)}, u32[]{:S(2)}) copy-start(pred[4]{0:T(512)(128)(4,1)} %get-tuple-element.97) | copy-start | bytes 16
  76.1 12.4 %copy-start.17 = (pred[4]{0:T(512)(128)(4,1)S(1)}, pred[4]{0:T(512)(128)(4,1)}, u32[]{:S(2)}) copy-start(pred[4]{0:T(512)(128)(4,1)} %get-tuple-element.40) | copy-start | bytes 16
  76.1 12.4 %copy-start.18 = (pred[4]{0:T(512)(128)(4,1)S(1)}, pred[4]{0:T(512)(128)(4,1)}, u32[]{:S(2)}) copy-start(pred[4]{0:T(512)(128)(4,1)} %get-tuple-element.92) | copy-start | bytes 16
  76.1 12.4 %copy-start.19 = (pred[4]{0:T(512)(128)(4,1)S(1)}, pred[4]{0:T(512)(128)(4,1)}, u32[]{:S(2)}) copy-start(pred[4]{0:T(512)(128)(4,1)} %get-tuple-element.93) | copy-start | bytes 16
  76.1 12.5 %copy-start.14 = (pred[4]{0:T(512)(128)(4,1)S(1)}, pred[4]{0:T(512)(128)(4,1)}, u32[]{:S(2)}) copy-start(pred[4]{0:T(512)(128)(4,1)} %get-tuple-element.106) | copy-start | bytes 16
  76.1 12.5 %copy-start.15 = (pred[4]{0:T(512)(128)(4,1)S(1)}, pred[4]{0:T(512)(128)(4,1)}, u32[]{:S(2)}) copy-start(pred[4]{0:T(512)(128)(4,1)} %get-tuple-element.107) | copy-start | bytes 16
  76.1 12.5 %copy-start.16 = (pred[4]{0:T(512)(128)(4,1)S(1)}, pred[4]{0:T(512)(128)(4,1)}, u32[]{:S(2)}) copy-start(pred[4]{0:T(512)(128)(4,1)} %get-tuple-element.108) | copy-start | bytes 16
  77.0 7.0 %collective-permute-start.7 = (f32[1,4,4,6,256]{4,3,1,2,0:T(8,128)S(1)}, f32[1,4,4,6,256]{4,3,1,2,0:T(8,128)S(1)}, u32[]{:S(2)}, u32[]{:S(2)}) collective-permute-start(f32[1,4,4,6,256]{4,3,1,2,0:T(8,128)S(1)} %maximum_bitcast_fusion.1), channel_id=1, source_target_pairs={{0,1},{1,2},{2,3},{3,4},{4,5},{5,6},{6,7},{7,8},{8,9},{9,10},{10,1... | collective-permute-start | bytes 294920 | tf_op jit(solution)/shard_map/ppermute | solution.py:25
  78.9 6.3 %collective-permute-start.6 = (f32[1,4,4,6,256]{4,3,1,2,0:T(8,128)S(1)}, f32[1,4,4,6,256]{4,3,1,2,0:T(8,128)S(1)}, u32[]{:S(2)}, u32[]{:S(2)}) collective-permute-start(f32[1,4,4,6,256]{4,3,1,2,0:T(8,128)S(1)} %maximum_bitcast_fusion.1), channel_id=1, source_target_pairs={{1,0},{2,1},{3,2},{4,3},{5,4},{6,5},{7,6},{8,7},{9,8},{10,9},{11,1... | collective-permute-start | bytes 294920 | tf_op jit(solution)/shard_map/ppermute | solution.py:28
  89.5 15.5 %copy-start.11 = (pred[4]{0:T(512)(128)(4,1)S(1)}, pred[4]{0:T(512)(128)(4,1)}, u32[]{:S(2)}) copy-start(pred[4]{0:T(512)(128)(4,1)} %get-tuple-element.46) | copy-start | bytes 16
  89.5 15.5 %copy-start.12 = (pred[4]{0:T(512)(128)(4,1)S(1)}, pred[4]{0:T(512)(128)(4,1)}, u32[]{:S(2)}) copy-start(pred[4]{0:T(512)(128)(4,1)} %get-tuple-element.98) | copy-start | bytes 16
  89.5 15.5 %copy-start.13 = (pred[4]{0:T(512)(128)(4,1)S(1)}, pred[4]{0:T(512)(128)(4,1)}, u32[]{:S(2)}) copy-start(pred[4]{0:T(512)(128)(4,1)} %get-tuple-element.99) | copy-start | bytes 16
  89.5 16.2 %copy-start.2 = (pred[4]{0:T(512)(128)(4,1)S(1)}, pred[4]{0:T(512)(128)(4,1)}, u32[]{:S(2)}) copy-start(pred[4]{0:T(512)(128)(4,1)} %get-tuple-element.48) | copy-start | bytes 16
  89.5 16.2 %copy-start.3 = (pred[4]{0:T(512)(128)(4,1)S(1)}, pred[4]{0:T(512)(128)(4,1)}, u32[]{:S(2)}) copy-start(pred[4]{0:T(512)(128)(4,1)} %get-tuple-element.100) | copy-start | bytes 16
  89.6 16.2 %copy-start.4 = (pred[4]{0:T(512)(128)(4,1)S(1)}, pred[4]{0:T(512)(128)(4,1)}, u32[]{:S(2)}) copy-start(pred[4]{0:T(512)(128)(4,1)} %get-tuple-element.101) | copy-start | bytes 16
  94.6 6.7 %collective-permute-start.9 = (f32[1,4,2,6,256]{4,3,1,2,0:T(8,128)S(1)}, f32[1,4,2,6,256]{4,3,1,2,0:T(8,128)S(1)}, u32[]{:S(2)}, u32[]{:S(2)}) collective-permute-start(f32[1,4,2,6,256]{4,3,1,2,0:T(8,128)S(1)} %maximum_bitcast_fusion.3), channel_id=1, source_target_pairs={{0,64},{64,128},{128,192},{192,256},{256,320},{320,384},{384,448},... | collective-permute-start | bytes 147464 | tf_op jit(solution)/shard_map/ppermute | solution.py:25
  99.0 5.3 %collective-permute-start.8 = (f32[1,4,2,6,256]{4,3,1,2,0:T(8,128)S(1)}, f32[1,4,2,6,256]{4,3,1,2,0:T(8,128)S(1)}, u32[]{:S(2)}, u32[]{:S(2)}) collective-permute-start(f32[1,4,2,6,256]{4,3,1,2,0:T(8,128)S(1)} %maximum_bitcast_fusion.3), channel_id=1, source_target_pairs={{64,0},{128,64},{192,128},{256,192},{320,256},{384,320},{448,384},... | collective-permute-start | bytes 147464 | tf_op jit(solution)/shard_map/ppermute | solution.py:28
  111.1 5.0 %copy-start.30 = (pred[256]{0:T(512)(128)(4,1)S(1)}, pred[256]{0:T(512)(128)(4,1)}, u32[]{:S(2)}) copy-start(pred[256]{0:T(512)(128)(4,1)} %get-tuple-element.110) | copy-start | bytes 772
  111.1 5.0 %copy-start.31 = (pred[256]{0:T(512)(128)(4,1)S(1)}, pred[256]{0:T(512)(128)(4,1)}, u32[]{:S(2)}) copy-start(pred[256]{0:T(512)(128)(4,1)} %get-tuple-element.111) | copy-start | bytes 772
  113.2 3.4 %copy-start.29 = (f32[2]{0:T(128)S(1)}, f32[2]{0:T(128)}, u32[]{:S(2)}) copy-start(f32[2]{0:T(128)} %constant.250.clone) | copy-start | bytes 28
  113.2 3.7 %copy-start.6 = (f32[4]{0:T(128)S(1)}, f32[4]{0:T(128)}, u32[]{:S(2)}) copy-start(f32[4]{0:T(128)} %get-tuple-element.87) | copy-start | bytes 52
  113.2 3.7 %copy-start.8 = (f32[4]{0:T(128)S(1)}, f32[4]{0:T(128)}, u32[]{:S(2)}) copy-start(f32[4]{0:T(128)} %get-tuple-element.88) | copy-start | bytes 52
  113.2 3.8 %copy-start.10 = (f32[4]{0:T(128)S(1)}, f32[4]{0:T(128)}, u32[]{:S(2)}) copy-start(f32[4]{0:T(128)} %get-tuple-element.89) | copy-start | bytes 52
  113.2 3.8 %copy-start.27 = (f32[4]{0:T(128)S(1)}, f32[4]{0:T(128)}, u32[]{:S(2)}) copy-start(f32[4]{0:T(128)} %constant.249.clone) | copy-start | bytes 52
where the time goes:
time: 119 us
  local copies, waits for them, and re-layouts  54.5 us (46%)
  starting transfers between devices  37.4 us (31%)
  other arithmetic  16.7 us (14%)
  waiting for transfers between devices  7.44 us (6%)
  between operations  2.63 us (2%)
    ppermute x2, starting transfers between devices, swapped(): return lax.ppermute(block, axis, route)  18 us
    ppermute x4, starting transfers between devices, padded(): lax.ppermute(lax.slice_in_dim(block, block.shape[dim] - width, None, axis...  11.4 us
    gather x12, local copies, waits for them, and re-layouts, one_step(): remote = jnp.take(remote_tables[face], slot_index, axis=0)  8.07 us
    ppermute x4, starting transfers between devices, padded(): lax.ppermute(lax.slice_in_dim(block, 0, width, axis=dim), axis, backward)  7.94 us
    gather x12, local copies, waits for them, and re-layouts, one_step(): local = jnp.take(table[:, opposite], slot_index, axis=0)  7.83 us
    reshape x2, local copies, waits for them, and re-layouts, one_step(): wall_high_z = jnp.broadcast_to(ghosts[5].reshape(slots, nfield, edge, edg...  5.61 us
    reshape x2, local copies, waits for them, and re-layouts, one_step(): wall_low_z = jnp.broadcast_to(ghosts[4].reshape(slots, nfield, edge, edge...  5.59 us
    slice x4, local copies, waits for them, and re-layouts, face_table(): upper_z = state[:, :, :, edge - 1::edge].reshape(slots, nfield, plane)  4.72 us
  transfers between devices with their start and end apart: 10, of which 3 were waited for; matrix products, arithmetic and copies ran while one was open for 29% of the time, Pallas kernels for 0%

commit v1 on v0

v1 whole, which is shorter than its diff:
```python
import functools
import math

import jax
import jax.numpy as jnp
import numpy as np
from jax import lax
from jax.experimental import pallas as pl
from jax.experimental.pallas import tpu as pltpu
from jax.sharding import PartitionSpec as P

MESH = pl.DeviceIdType.MESH
NORI = 8
EDGE = 16
SLOTS = 4
NFIELD = 6
LANES = 128
HALVES = 2
TILES = 3

phase_rate = 0.05
closure = 0.1
conc_rates = (0.08, 0.04)


def roll(v, shift, axis):
    shift %= v.shape[axis]
    return v if shift == 0 else pltpu.roll(v, shift, axis)


def rows_of(ref, half, tile, x):
    start = half * (NFIELD * SLOTS * EDGE) + tile * (8 * EDGE) + x
    flat = ref.reshape(HALVES * NFIELD * SLOTS * EDGE, LANES)
    return flat, pl.ds(start, 8, stride=EDGE)


def read_rows(ref, half, tile, x):
    flat, rows = rows_of(ref, half, tile, x)
    return flat[rows, :]


def write_rows(ref, half, tile, x, v):
    flat, rows = rows_of(ref, half, tile, x)
    flat[rows, :] = v


def kernel(
    n_grp, n_dev, fields, swap_dev, swap_grp, neighbors, orient, out,
    raw, moved, state0, state1, result, faces0, faces1, ghosts0, ghosts1, chosen,
    load_sem, store_sem, move_send, move_recv, send_sem, recv_sem,
):
    grp, dev = lax.axis_index("grp"), lax.axis_index("dev")
    rank = grp * n_dev + dev
    above_dev, below_dev = lax.rem(dev + 1, n_dev), lax.rem(dev + n_dev - 1, n_dev)
    above_grp, below_grp = lax.rem(grp + 1, n_grp), lax.rem(grp + n_grp - 1, n_grp)
    pair_dev = dev + 1 - 2 * lax.rem(dev, 2)
    pair_grp = grp + 1 - 2 * lax.rem(grp, 2)

    loads = []
    for slot in range(SLOTS):
        for half in range(HALVES):
            loads.append(
                pltpu.make_async_copy(
                    fields.at[slot, :, :, pl.ds(half * LANES, LANES)],
                    raw.at[half, :, slot],
                    load_sem.at[slot * HALVES + half],
                )
            )
    for copy in loads:
        copy.start()

    barrier = pltpu.get_barrier_semaphore()
    for target in ({"dev": above_dev}, {"dev": below_dev}, {"grp": above_grp}, {"grp": below_grp}):
        pl.semaphore_signal(barrier, inc=1, device_id=target, device_id_type=MESH)
    pl.semaphore_wait(barrier, 4)

    moves = []
    for slot, target in ((0, {"grp": pair_grp}), (SLOTS - 1, {"dev": pair_dev})):
        for half in range(HALVES):
            index = len(moves)
            moves.append(
                pltpu.make_async_remote_copy(
                    src_ref=fields.at[slot, :, :, pl.ds(half * LANES, LANES)],
                    dst_ref=moved.at[half, :, slot],
                    send_sem=move_send.at[index],
                    recv_sem=move_recv.at[index],
                    device_id=target,
                    device_id_type=MESH,
                )
            )
    for copy in moves:
        copy.start()

    row = lax.broadcasted_iota(jnp.int32, (8, LANES), 0)
    lane = lax.broadcasted_iota(jnp.int32, (8, LANES), 1)
    slot_of = row & 3
    z = lane & 15
    column = lane >> 4
    lane3 = lax.broadcasted_iota(jnp.int32, (TILES, 8, LANES), 2)
    z3 = lane3 & 15
    column3 = lane3 >> 4

    def per_slot(scalars):
        last = jnp.full((8, LANES), scalars[SLOTS - 1])
        for slot in range(SLOTS - 1):
            last = jnp.where(slot_of == slot, scalars[slot], last)
        return last

    angle = per_slot([orient[slot] for slot in range(SLOTS)])
    cosine = jnp.zeros((8, LANES), jnp.float32)
    sine = jnp.zeros((8, LANES), jnp.float32)
    for number in range(NORI):
        theta = np.float32(math.pi) * np.float32(number) / np.float32(NORI)
        cosine = jnp.where(angle == number, jnp.float32(np.cos(np.float32(2.0) * theta)), cosine)
        sine = jnp.where(angle == number, jnp.float32(np.sin(np.float32(2.0) * theta)), sine)
    scale_x = phase_rate * (1.0 + 0.5 * cosine)
    scale_y = phase_rate * (1.0 - 0.5 * cosine)
    scale_z = phase_rate * (1.0 + 0.5 * sine)
    scale_c = jnp.where(row < 4, jnp.float32(conc_rates[0]), jnp.float32(conc_rates[1]))
    self_p = 1.0 - 2.0 * (scale_x + scale_y + scale_z)
    self_c = 1.0 - 6.0 * scale_c

    picks = []
    for face in range(6):
        target = per_slot([neighbors[slot, face] for slot in range(SLOTS)])
        source_row = (row & 4) | (target & 3)
        picks.append((target < 0, (target >> 2) == rank, source_row))

    swapped_here = ((slot_of == 0) & (swap_grp[0] == 1)) | (
        (slot_of == SLOTS - 1) & (swap_dev[0] == 1)
    )

    for copy in loads:
        copy.wait()
    for x in range(EDGE):
        for half in range(HALVES):
            for tile in range(TILES):
                state0[x, half, tile] = read_rows(raw, half, tile, x)
    for copy in moves:
        copy.wait_recv()

    def pack(x, half, v, packs):
        y_low, y_high, z_low, z_high = packs
        if half == 0:
            y_low[x // 8] = jnp.where(column3 == x % 8, roll(v, 16 * x, 2), y_low[x // 8])
        else:
            y_high[x // 8] = jnp.where(column3 == x % 8, roll(v, 16 * x + 16, 2), y_high[x // 8])
        z_low[half] = jnp.where(z3 == x, roll(v, x, 2), z_low[half])
        z_high[half] = jnp.where(z3 == x, roll(v, x - 15, 2), z_high[half])

    def new_packs():
        zero = jnp.zeros((TILES, 8, LANES), jnp.float32)
        return [[zero, zero] for _ in range(4)]

    def send_copies(state, faces, ghosts, first):
        plan = (
            (state.at[EDGE - 1], 0, {"dev": above_dev}),
            (state.at[0], 1, {"dev": below_dev}),
            (faces.at[1], 2, {"dev": above_dev}),
            (faces.at[0], 3, {"dev": below_dev}),
            (faces.at[3], 4, {"grp": above_grp}),
            (faces.at[2], 5, {"grp": below_grp}),
        )
        return [
            pltpu.make_async_remote_copy(
                src_ref=source,
                dst_ref=ghosts.at[into],
                send_sem=send_sem.at[first + into],
                recv_sem=recv_sem.at[first + into],
                device_id=target,
                device_id_type=MESH,
            )
            for source, into, target in plan
        ]

    def store_packs(packs, faces):
        for number, pair in enumerate(packs):
            for half in range(HALVES):
                faces[number, half] = pair[half]

    def choose(state, faces, ghosts, copies):
        own = (state.at[0], state.at[EDGE - 1], faces.at[0], faces.at[1], faces.at[2], faces.at[3])
        for face in range(6):
            copies[face].wait_recv()
            outer, local, source_row = picks[face]
            mine, opposite = own[face], own[face + 1 - 2 * (face % 2)]
            for half in range(HALVES):
                for tile in range(TILES):
                    near = jnp.take_along_axis(opposite[half, tile], source_row, axis=0)
                    far = jnp.take_along_axis(ghosts[face, half, tile], source_row, axis=0)
                    chosen[face, half, tile] = jnp.where(
                        outer, mine[half, tile], jnp.where(local, near, far)
                    )

    def advance(state, x, half):
        v = state[x, half]
        other = state[x, 1 - half]
        below = chosen[0, half] if x == 0 else state[x - 1, half]
        above = chosen[1, half] if x == EDGE - 1 else state[x + 1, half]
        sum_x = below + above
        if half == 0:
            up = jnp.where(lane3 < 16, other, v)
            down = jnp.where(lane3 >= 112, roll(chosen[2, x // 8], 112 - 16 * x, 2), v)
        else:
            up = jnp.where(lane3 < 16, roll(chosen[3, x // 8], -16 * x, 2), v)
            down = jnp.where(lane3 >= 112, other, v)
        sum_y = roll(up, -16, 2) + roll(down, 16, 2)
        sum_z = jnp.where(z3 == 15, roll(chosen[5, half], 15 - x, 2), roll(v, -1, 2)) + jnp.where(
            z3 == 0, roll(chosen[4, half], -x, 2), roll(v, 1, 2)
        )
        p, c = v[:2], v[2]
        linear = scale_x * sum_x[:2] + scale_y * sum_y[:2] + scale_z * sum_z[:2] + self_p * p
        new_c = scale_c * (sum_x[2] + sum_y[2] + sum_z[2]) + self_c * c
        both = p[0] + p[1]
        total = both + roll(both, 4, 0)
        drive = c - roll(c, 4, 0)
        shared = (phase_rate * closure) - (phase_rate * closure) * total
        well = p - p * p
        bend = 2.0 * phase_rate * p - phase_rate
        new_0 = linear[0] + shared + well[0] * (bend[0] + (0.5 * phase_rate) * drive)
        new_1 = linear[1] + shared + well[1] * (bend[1] + phase_rate * drive)
        return new_0, new_1, new_c

    packs = new_packs()
    for x in range(EDGE):
        for half in range(HALVES):
            tiles = []
            for tile in range(TILES):
                arrived = read_rows(moved, half, tile, x)
                tiles.append(jnp.where(swapped_here, arrived, state0[x, half, tile]))
            v = jnp.stack(tiles)
            state0[x, half] = v
            pack(x, half, v, packs)
    store_packs(packs, faces0)
    first = send_copies(state0, faces0, ghosts0, 0)
    for copy in first:
        copy.start()
    choose(state0, faces0, ghosts0, first)

    packs = new_packs()
    for x in range(EDGE):
        for half in range(HALVES):
            v = jnp.stack(advance(state0, x, half))
            state1[x, half] = v
            pack(x, half, v, packs)
    store_packs(packs, faces1)
    second = send_copies(state1, faces1, ghosts1, 6)
    for copy in second:
        copy.start()
    choose(state1, faces1, ghosts1, second)

    stores = []
    for half in range(HALVES):
        for x in range(EDGE):
            for tile, v in enumerate(advance(state1, x, half)):
                write_rows(result, half, tile, x, v)
        for slot in range(SLOTS):
            stores.append(
                pltpu.make_async_copy(
                    result.at[half, :, slot],
                    out.at[slot, :, :, pl.ds(half * LANES, LANES)],
                    store_sem.at[half * SLOTS + slot],
                )
            )
            stores[-1].start()
    for copy in stores:
        copy.wait()
    for copy in moves + first + second:
        copy.wait_send()


def solution(mesh):
    n_grp, n_dev = mesh.shape["grp"], mesh.shape["dev"]

    def body(fields, swap_dev, swap_grp, neighbors, orient):
        block = (HALVES, NFIELD, SLOTS, EDGE, LANES)
        cells = (EDGE, HALVES, TILES, 8, LANES)
        return pl.pallas_call(
            functools.partial(kernel, n_grp, n_dev),
            out_shape=jax.ShapeDtypeStruct(fields.shape, fields.dtype),
            in_specs=[pl.BlockSpec(memory_space=pltpu.HBM)]
            + [pl.BlockSpec(memory_space=pltpu.SMEM)] * 4,
            out_specs=pl.BlockSpec(memory_space=pl.ANY),
            scratch_shapes=[
                pltpu.VMEM(block, jnp.float32),
                pltpu.VMEM(block, jnp.float32),
                pltpu.VMEM(cells, jnp.float32),
                pltpu.VMEM(cells, jnp.float32),
                pltpu.VMEM(block, jnp.float32),
                pltpu.VMEM((4,) + cells[1:], jnp.float32),
                pltpu.VMEM((4,) + cells[1:], jnp.float32),
                pltpu.VMEM((6,) + cells[1:], jnp.float32),
                pltpu.VMEM((6,) + cells[1:], jnp.float32),
                pltpu.VMEM((6,) + cells[1:], jnp.float32),
                pltpu.SemaphoreType.DMA((8,)),
                pltpu.SemaphoreType.DMA((8,)),
                pltpu.SemaphoreType.DMA((4,)),
                pltpu.SemaphoreType.DMA((4,)),
                pltpu.SemaphoreType.DMA((12,)),
                pltpu.SemaphoreType.DMA((12,)),
            ],
            compiler_params=pltpu.CompilerParams(
                collective_id=0, has_side_effects=True, vmem_limit_bytes=16 * 2**20
            ),
            name="phase_field_steps",
        )(fields, swap_dev, swap_grp, neighbors, orient)

    in_specs = (
        P(("grp", "dev"), None, None, None),
        P(("grp", "dev")),
        P(("grp", "dev")),
        P(("grp", "dev"), None),
        P(("grp", "dev")),
    )
    out_specs = P(("grp", "dev"), None, None, None)
    return jax.shard_map(body, mesh=mesh, in_specs=in_specs, out_specs=out_specs, check_vma=False)
```

time: 119 us -> 40.5 us (0.34)
  local copies, waits for them, and re-layouts: 54.5 us -> 1.75 us
  starting transfers between devices: 37.4 us -> 0 us
  Pallas kernels: 0 us -> 37.2 us
  other arithmetic: 16.7 us -> 0 us
  waiting for transfers between devices: 7.44 us -> 0 us
  between operations: 2.63 us -> 1.37 us
    ppermute x10 -> x0, starting transfers between devices: 37.4 us -> none  [the longest x2 18 us: swapped(): return lax.ppermute(block, axis, route)]
    pallas_call x0 -> x1, Pallas kernels: none -> 37.2 us  [body(): pl.pallas_call(functools.partial(kernel, n_grp, n_dev), out_shape=jax.Sha...]
    gather x24 -> x0, local copies, waits for them, and re-layouts: 15.9 us -> none  [the longest x12 8.07 us: one_step(): remote = jnp.take(remote_tables[face], slot_index, axis=0)]
    slice x16 -> x0, local copies, waits for them, and re-layouts: 12.2 us -> none  [the longest x4 4.72 us: face_table(): upper_z = state[:, :, :, edge - 1::edge].reshape(slots, nfield, plane)]
    reshape x12 -> x0, local copies, waits for them, and re-layouts: 11.9 us -> none  [the longest x2 5.61 us: one_step(): wall_high_z = jnp.broadcast_to(ghosts[5].reshape(slots, nfield, edge, edg...]
    broadcast_in_dim x8 -> x0, local copies, waits for them, and re-layouts: 8.97 us -> none  [the longest x4 4.48 us: one_step(): jnp.broadcast_to(ghosts[4].reshape(slots, nfield, edge, edge, 1), (slots,...]
    ppermute x10 -> x0, waiting for transfers between devices: 7.44 us -> none  [the longest x2 4.53 us: swapped(): return lax.ppermute(block, axis, route)]
    add x8 -> x0, other arithmetic: 5.26 us -> none  [the longest x2 1.72 us: one_step(): sum_z = above + below]
  transfers between devices with their start and end apart: 10 -> 0, of which waited for: 3 -> 0; matrix products, arithmetic and copies ran while one was open for 29% -> 0% of each run, Pallas kernels for 0% -> 0%
where the time goes in v1:
time: 40.5 us; the launch traced here: 40.3 us
  Pallas kernels  37.2 us (92%)
  local copies, waits for them, and re-layouts  1.75 us (4%)
  between operations  1.37 us (3%)
    pallas_call x1, Pallas kernels, body(): pl.pallas_call(functools.partial(kernel, n_grp, n_dev), out_shape=jax.Sha...  37.2 us
    unnamed x7, local copies, waits for them, and re-layouts  1.75 us

profile of v1, /device:TPU:1, one launch (start us, length us, event | category | flops | bytes accessed | tf_op | source)
XLA Modules:
  0.0 40.3 jit_solution(9984615441652736569)
XLA Ops:
  0.0 0.0 copy-start.1
  0.7 0.0 copy-start.2
  1.3 0.0 copy-done.1
  1.3 0.0 copy-done.2
  1.4 0.0 copy-start
  1.4 1.0 %copy-done = f32[4,6,16,256]{3,2,1,0:T(8,128)S(1)} copy-done((f32[4,6,16,256]{3,2,1,0:T(8,128)S(1)}, f32[4,6,16,256]{3,2,1,0:T(8,128)}, u32[]{:S(2)}) %copy-start) | copy-done | bytes 393240
  2.4 37.2 %phase_field_steps.1 = f32[4,6,16,256]{3,2,1,0:T(8,128)S(1)} custom-call(f32[4,6,16,256]{3,2,1,0:T(8,128)S(1)} %copy-done, s32[1]{0:T(128)S(6)} %copy.7.swap_dev, s32[1]{0:T(128)S(6)} %copy.8.swap_grp, s32[4,6]{1,0:T(4,128)S(1)} %copy-done.1, s32[4]{0:T(128)S(1)} %copy-done.2), custom_call_target="tpu_custom_call" | custom-call | tf_op jit(solution)/shard_map/phase_field_steps/pallas_call | solution.py:278
  39.5 0.7 %copy.9 = f32[4,6,16,256]{3,2,1,0:T(8,128)} copy(f32[4,6,16,256]{3,2,1,0:T(8,128)S(1)} %phase_field_steps.1) | data formatting | bytes 786432
Async XLA Ops:
  0.0 1.3 %copy-start.1 = (s32[4,6]{1,0:T(4,128)S(1)}, s32[4,6]{1,0:T(4,128)}, u32[]{:S(2)}) copy-start(s32[4,6]{1,0:T(4,128)} %neighbors.1) | copy-start | bytes 292
  0.7 0.7 %copy-start.2 = (s32[4]{0:T(128)S(1)}, s32[4]{0:T(128)}, u32[]{:S(2)}) copy-start(s32[4]{0:T(128)} %orient.1) | copy-start | bytes 52
  1.4 1.0 %copy-start = (f32[4,6,16,256]{3,2,1,0:T(8,128)S(1)}, f32[4,6,16,256]{3,2,1,0:T(8,128)}, u32[]{:S(2)}) copy-start(f32[4,6,16,256]{3,2,1,0:T(8,128)} %fields.1) | copy-start | bytes 1179652

commit v2 on v1

v2 whole, which is shorter than its diff:
```python
import functools
import math

import jax
import jax.numpy as jnp
import numpy as np
from jax import lax
from jax.experimental import pallas as pl
from jax.experimental.pallas import tpu as pltpu
from jax.sharding import PartitionSpec as P

MESH = pl.DeviceIdType.MESH
NORI = 8
EDGE = 16
SLOTS = 4
NFIELD = 6
LANES = 128
HALVES = 2
TILES = 3

phase_rate = 0.05
closure = 0.1
conc_rates = (0.08, 0.04)


def in_hbm(a):
    return pltpu.with_memory_space_constraint(a, pltpu.HBM)


def roll(v, shift):
    shift %= LANES
    return v if shift == 0 else pltpu.roll(v, shift, v.ndim - 1)


def rows_of(ref, half, tile, x):
    start = half * (NFIELD * SLOTS * EDGE) + tile * (8 * EDGE) + x
    flat = ref.reshape(HALVES * NFIELD * SLOTS * EDGE, LANES)
    return flat, pl.ds(start, 8, stride=EDGE)


def read_rows(ref, half, tile, x):
    flat, rows = rows_of(ref, half, tile, x)
    return flat[rows, :]


def write_rows(ref, half, tile, x, v):
    flat, rows = rows_of(ref, half, tile, x)
    flat[rows, :] = v


def kernel(
    n_grp, n_dev, fields, swap_dev, swap_grp, neighbors_hbm, orient_hbm, out,
    neighbors, orient,
    raw, moved, state0, state1, partial, result, faces0, faces1, ghosts0, ghosts1, chosen, walls_y, walls_z,
    small_sem, load_sem, store_sem, move_send, move_recv, send_sem, recv_sem,
):
    grp, dev = lax.axis_index("grp"), lax.axis_index("dev")
    rank = grp * n_dev + dev
    pair_dev = dev + 1 - 2 * lax.rem(dev, 2)
    pair_grp = grp + 1 - 2 * lax.rem(grp, 2)
    has_below_dev, has_above_dev = dev > 0, dev < n_dev - 1
    has_below_grp, has_above_grp = grp > 0, grp < n_grp - 1
    sides = (
        (has_below_dev, {"dev": dev - 1}),
        (has_above_dev, {"dev": dev + 1}),
        (has_below_grp, {"grp": grp - 1}),
        (has_above_grp, {"grp": grp + 1}),
    )

    barrier = pltpu.get_barrier_semaphore()
    for there, target in sides:

        @pl.when(there)
        def _():
            pl.semaphore_signal(barrier, inc=1, device_id=target, device_id_type=MESH)

    smalls = [
        pltpu.make_async_copy(source, into, small_sem.at[number])
        for number, (source, into) in enumerate(
            (
                (neighbors_hbm, neighbors),
                (orient_hbm, orient),
            )
        )
    ]
    loads = []
    for half in range(HALVES):
        for slot in range(SLOTS):
            loads.append(
                pltpu.make_async_copy(
                    fields.at[slot, :, :, pl.ds(half * LANES, LANES)],
                    raw.at[half, :, slot],
                    load_sem.at[half * SLOTS + slot],
                )
            )
    for copy in smalls + loads:
        copy.start()
    peers = [jnp.where(there, 1, 0) for there, _ in sides]
    pl.semaphore_wait(barrier, peers[0] + peers[1] + peers[2] + peers[3])

    moves = []
    for slot, target in ((0, {"grp": pair_grp}), (SLOTS - 1, {"dev": pair_dev})):
        for half in range(HALVES):
            index = len(moves)
            moves.append(
                pltpu.make_async_remote_copy(
                    src_ref=fields.at[slot, :, :, pl.ds(half * LANES, LANES)],
                    dst_ref=moved.at[half, :, slot],
                    send_sem=move_send.at[index],
                    recv_sem=move_recv.at[index],
                    device_id=target,
                    device_id_type=MESH,
                )
            )
    for copy in moves:
        copy.start()

    row = lax.broadcasted_iota(jnp.int32, (8, LANES), 0)
    lane = lax.broadcasted_iota(jnp.int32, (8, LANES), 1)
    slot_of = row & 3
    z = lane & 15
    column = lane >> 4
    low_y, high_y = lane < EDGE, lane >= LANES - EDGE

    def per_slot(scalars):
        last = jnp.full((8, LANES), scalars[SLOTS - 1])
        for slot in range(SLOTS - 1):
            last = jnp.where(slot_of == slot, scalars[slot], last)
        return last

    for copy in smalls:
        copy.wait()
    angle = per_slot([orient[slot] for slot in range(SLOTS)])
    cosine = jnp.zeros((8, LANES), jnp.float32)
    sine = jnp.zeros((8, LANES), jnp.float32)
    for number in range(NORI):
        theta = np.float32(math.pi) * np.float32(number) / np.float32(NORI)
        cosine = jnp.where(angle == number, jnp.float32(np.cos(np.float32(2.0) * theta)), cosine)
        sine = jnp.where(angle == number, jnp.float32(np.sin(np.float32(2.0) * theta)), sine)
    scale_x = phase_rate * (1.0 + 0.5 * cosine)
    scale_y = phase_rate * (1.0 - 0.5 * cosine)
    scale_z = phase_rate * (1.0 + 0.5 * sine)
    scale_c = jnp.where(row < 4, jnp.float32(conc_rates[0]), jnp.float32(conc_rates[1]))
    self_p = 1.0 - 2.0 * (scale_x + scale_y + scale_z)
    self_c = 1.0 - 6.0 * scale_c
    zero = jnp.zeros((8, LANES), jnp.float32)
    scales_x = (scale_x, scale_x, scale_c)
    scales_y = tuple(
        tuple(jnp.where(wall, v, zero) for v in (scale_y, scale_y, scale_c)) for wall in (low_y, high_y)
    )
    scales_z = tuple(jnp.where((z == 0) | (z == EDGE - 1), v, zero) for v in (scale_z, scale_z, scale_c))

    picks = []
    for face in range(6):
        target = per_slot([neighbors[slot, face] for slot in range(SLOTS)])
        source_row = (row & 4) | (target & 3)
        picks.append((target < 0, (target >> 2) == rank, source_row))

    swapped_here = ((slot_of == 0) & (swap_grp[0] == 1)) | (
        (slot_of == SLOTS - 1) & (swap_dev[0] == 1)
    )

    def pack_y(state, faces):
        for side in range(2):
            for tile in range(TILES):
                low, high = zero, zero
                for k in range(8):
                    x = side * 8 + k
                    both = jnp.where(lane < 64, state[x, 0, tile], state[x, 1, tile])
                    turned = roll(both, 16 * k)
                    low = jnp.where(column == k, turned, low)
                    high = jnp.where(column == (k + 7) % 8, turned, high)
                faces[0, side, tile] = low
                faces[1, side, tile] = roll(high, 16)

    def pack_z(state, faces):
        for half in range(HALVES):
            for tile in range(TILES):
                low, high = zero, zero
                for x in range(EDGE):
                    turned = roll(state[x, half, tile], x)
                    low = jnp.where(z == x, turned, low)
                    high = jnp.where(z == (x + 15) % 16, turned, high)
                faces[2, half, tile] = low
                faces[3, half, tile] = roll(high, -15)

    def exchange(state, faces, ghosts, first):
        plan = (
            (state.at[EDGE - 1], 0, 1),
            (state.at[0], 1, 0),
            (faces.at[1], 2, 1),
            (faces.at[0], 3, 0),
            (faces.at[3], 4, 3),
            (faces.at[2], 5, 2),
        )
        return [
            (
                pltpu.make_async_remote_copy(
                    src_ref=source,
                    dst_ref=ghosts.at[into],
                    send_sem=send_sem.at[first + into],
                    recv_sem=recv_sem.at[first + into],
                    device_id=sides[side][1],
                    device_id_type=MESH,
                ),
                sides[side][0],
                sides[side ^ 1][0],
            )
            for source, into, side in plan
        ]

    def start(copies):
        for copy, there, _ in copies:

            @pl.when(there)
            def _():
                copy.start()

    def choose(state, faces, ghosts, copies):
        own = (state.at[0], state.at[EDGE - 1], faces.at[0], faces.at[1], faces.at[2], faces.at[3])
        for copy, _, comes in copies:

            @pl.when(comes)
            def _():
                copy.wait_recv()

        def pick(face, part, tile):
            outer, local, source_row = picks[face]
            near = jnp.take_along_axis(own[face ^ 1][part, tile], source_row, axis=0)
            far = jnp.take_along_axis(ghosts[face, part, tile], source_row, axis=0)
            return jnp.where(outer, own[face][part, tile], jnp.where(local, near, far))

        for part in range(2):
            for tile in range(TILES):
                chosen[0, part, tile] = pick(0, part, tile)
                chosen[1, part, tile] = pick(1, part, tile)
                below, above = roll(pick(2, part, tile), 16), pick(3, part, tile)
                walls_y[0, part, tile] = jnp.where(column % 2 == 0, above, below)
                walls_y[1, part, tile] = jnp.where(column % 2 == 1, above, below)
                below, above = roll(pick(4, part, tile), -15), pick(5, part, tile)
                walls_z[0, part, tile] = jnp.where(z % 2 == 0, above, below)
                walls_z[1, part, tile] = jnp.where(z % 2 == 1, above, below)

    def prepare(state, x):
        v = [[state[x, half, tile] for tile in range(TILES)] for half in range(HALVES)]
        linear = [[None] * TILES for _ in range(HALVES)]
        for tile in range(TILES):
            ups = [roll(v[half][tile], -16) for half in range(HALVES)]
            downs = [roll(v[half][tile], 16) for half in range(HALVES)]
            sums_y = (
                jnp.where(high_y, ups[1], ups[0]) + jnp.where(low_y, zero, downs[0]),
                jnp.where(high_y, zero, ups[1]) + jnp.where(low_y, downs[0], downs[1]),
            )
            for half in range(HALVES):
                sum_z = jnp.where(z == EDGE - 1, zero, roll(v[half][tile], -1)) + jnp.where(
                    z == 0, zero, roll(v[half][tile], 1)
                )
                inner = [state[n, half, tile] for n in (x - 1, x + 1) if 0 <= n < EDGE]
                sum_x = inner[0] + inner[1] if len(inner) == 2 else inner[0]
                if tile < 2:
                    linear[half][tile] = (
                        scale_x * sum_x + scale_y * sums_y[half] + scale_z * sum_z + self_p * v[half][tile]
                    )
                else:
                    linear[half][tile] = scale_c * (sum_x + sums_y[half] + sum_z) + self_c * v[half][tile]
        for half in range(HALVES):
            p, q, c = v[half]
            both = p + q
            total = both + pltpu.roll(both, 4, 0)
            drive = c - pltpu.roll(c, 4, 0)
            shared = (phase_rate * closure) - (phase_rate * closure) * total
            partial[x, half, 0] = (
                linear[half][0]
                + shared
                + (p - p * p) * (2.0 * phase_rate * p - phase_rate + (0.5 * phase_rate) * drive)
            )
            partial[x, half, 1] = (
                linear[half][1]
                + shared
                + (q - q * q) * (2.0 * phase_rate * q - phase_rate + phase_rate * drive)
            )
            partial[x, half, 2] = linear[half][2]

    def finish(x, half, tile):
        v = partial[x, half, tile]
        v = v + scales_z[tile] * roll(walls_z[x % 2, half, tile], 15 - x)
        v = v + scales_y[half][tile] * roll(walls_y[x % 2, x // 8, tile], 16 * (7 - x % 8))
        if x == 0:
            v = v + scales_x[tile] * chosen[0, half, tile]
        if x == EDGE - 1:
            v = v + scales_x[tile] * chosen[1, half, tile]
        return v

    for copy in loads:
        copy.wait()
    for x in range(EDGE):
        for half in range(HALVES):
            for tile in range(TILES):
                state0[x, half, tile] = read_rows(raw, half, tile, x)
    for copy in moves:
        copy.wait_recv()
    order = (0, EDGE - 1, *range(1, EDGE - 1))
    for x in order:
        for half in range(HALVES):
            for tile in range(TILES):
                state0[x, half, tile] = jnp.where(
                    swapped_here, read_rows(moved, half, tile, x), state0[x, half, tile]
                )

    first = exchange(state0, faces0, ghosts0, 0)
    start(first[:2])
    pack_z(state0, faces0)
    start(first[4:])
    pack_y(state0, faces0)
    start(first[2:4])
    for x in range(EDGE):
        prepare(state0, x)
    choose(state0, faces0, ghosts0, first)

    for x in order:
        for half in range(HALVES):
            for tile in range(TILES):
                state1[x, half, tile] = finish(x, half, tile)
    second = exchange(state1, faces1, ghosts1, 6)
    start(second[:2])
    pack_z(state1, faces1)
    start(second[4:])
    pack_y(state1, faces1)
    start(second[2:4])
    for x in range(EDGE):
        prepare(state1, x)
    choose(state1, faces1, ghosts1, second)

    stores = []
    for half in range(HALVES):
        for x in range(EDGE):
            for tile in range(TILES):
                write_rows(result, half, tile, x, finish(x, half, tile))
        for slot in range(SLOTS):
            stores.append(
                pltpu.make_async_copy(
                    result.at[half, :, slot],
                    out.at[slot, :, :, pl.ds(half * LANES, LANES)],
                    store_sem.at[half * SLOTS + slot],
                )
            )
            stores[-1].start()
    for copy in stores:
        copy.wait()
    for copy in moves:
        copy.wait_send()
    for copy, there, _ in first + second:

        @pl.when(there)
        def _():
            copy.wait_send()


def solution(mesh):
    n_grp, n_dev = mesh.shape["grp"], mesh.shape["dev"]

    def body(fields, swap_dev, swap_grp, neighbors, orient):
        block = (HALVES, NFIELD, SLOTS, EDGE, LANES)
        plane = (HALVES, TILES, 8, LANES)
        smalls = (neighbors, orient)
        shapes = [block, block] + [(EDGE,) + plane] * 3 + [block]
        shapes += [(4,) + plane, (4,) + plane, (6,) + plane, (6,) + plane] + [(2,) + plane] * 3
        return pl.pallas_call(
            functools.partial(kernel, n_grp, n_dev),
            out_shape=jax.ShapeDtypeStruct(fields.shape, fields.dtype),
            in_specs=[pl.BlockSpec(memory_space=space) for space in (pl.ANY, pltpu.SMEM, pltpu.SMEM, pl.ANY, pl.ANY)],
            out_specs=pl.BlockSpec(memory_space=pl.ANY),
            scratch_shapes=[pltpu.SMEM(a.shape, a.dtype) for a in smalls]
            + [pltpu.VMEM(shape, jnp.float32) for shape in shapes]
            + [pltpu.SemaphoreType.DMA((n,)) for n in (2, 8, 8, 4, 4, 12, 12)],
            compiler_params=pltpu.CompilerParams(
                collective_id=0, has_side_effects=True, vmem_limit_bytes=16 * 2**20
            ),
            name="phase_field_steps",
        )(
            in_hbm(fields), swap_dev, swap_grp, *[in_hbm(a) for a in smalls]
        )

    in_specs = (
        P(("grp", "dev"), None, None, None),
        P(("grp", "dev")),
        P(("grp", "dev")),
        P(("grp", "dev"), None),
        P(("grp", "dev")),
    )
    out_specs = P(("grp", "dev"), None, None, None)
    return jax.shard_map(body, mesh=mesh, in_specs=in_specs, out_specs=out_specs, check_vma=False)
```

time: 40.5 us -> 28 us (0.69)
  Pallas kernels: 37.2 us -> 25.8 us
  local copies, waits for them, and re-layouts: 1.75 us -> 0.75 us
    pallas_call x1, Pallas kernels: 37.2 us -> 25.8 us  [body(): pl.pallas_call(functools.partial(kernel, n_grp, n_dev), out_shape=jax.Sha...]
    unnamed x7 -> x1, local copies, waits for them, and re-layouts: 1.75 us -> 0.75 us
where the time goes in v2:
time: 28 us; the launch traced here: 27.8 us
  Pallas kernels  25.8 us (92%)
  between operations  1.3 us (5%)
  local copies, waits for them, and re-layouts  0.75 us (3%)
    pallas_call x1, Pallas kernels, body(): pl.pallas_call(functools.partial(kernel, n_grp, n_dev), out_shape=jax.Sha...  25.8 us
    unnamed x1, local copies, waits for them, and re-layouts  0.75 us

profile of v2, /device:TPU:1, one launch (start us, length us, event | category | flops | bytes accessed | tf_op | source)
XLA Modules:
  0.0 27.8 jit_solution(1315061036017150125)
XLA Ops:
  1.3 25.8 %phase_field_steps.1 = f32[4,6,16,256]{3,2,1,0:T(8,128)S(1)} custom-call(f32[4,6,16,256]{3,2,1,0:T(8,128)} %fields.1, s32[1]{0:T(128)S(6)} %copy.7.swap_dev, s32[1]{0:T(128)S(6)} %copy.8.swap_grp, s32[4,6]{1,0:T(4,128)} %neighbors_hbm.1, s32[4]{0:T(128)} %orient_hbm.1), custom_call_target="tpu_custom_call" | custom-call | tf_op jit(solution)/shard_map/phase_field_steps/pallas_call | solution.py:368
  27.1 0.7 %copy.9 = f32[4,6,16,256]{3,2,1,0:T(8,128)} copy(f32[4,6,16,256]{3,2,1,0:T(8,128)S(1)} %phase_field_steps.1) | data formatting | bytes 786432

commit v3 on v2

--- a/solution.py
+++ b/solution.py
@@ -43,45 +43,90 @@
     return flat[rows, :]
 
 
+def read_moved(moved, passed, odd, half, tile, x):
+    last = read_rows(moved, half, tile, x)
+    blocks = passed.reshape(2 * HALVES * NFIELD * EDGE, LANES)
+    start = (odd * HALVES + half) * (NFIELD * EDGE) + 2 * tile * EDGE + x
+    row = lax.broadcasted_iota(jnp.int32, (8, LANES), 0)
+    upper = jnp.broadcast_to(blocks[pl.ds(start, 1), :], (8, LANES))
+    lower = jnp.broadcast_to(blocks[pl.ds(start + EDGE, 1), :], (8, LANES))
+    return jnp.where(row == 0, upper, jnp.where(row == 4, lower, last))
+
+
 def write_rows(ref, half, tile, x, v):
-    flat, rows = rows_of(ref, half, tile, x)
-    flat[rows, :] = v
+    flat = ref.reshape(HALVES * NFIELD * SLOTS * EDGE, LANES)
+    for part in range(2):
+        start = (2 * tile + part) * 32 + (x // 8) * 16 + half * 8 + x % 8
+        flat[pl.ds(start, 4, stride=NFIELD * 32), :] = v[4 * part : 4 * part + 4]
+
+
+FACE_AT = (0, 13, 6, 19, 26, 35)
+FLAGS_AT = (12, 25, 32, 41)
+Z_BLOCK_AT = (33, 42)
+FIRST_AT, LAST_AT = 44, 56
+SHORT_AT = (0, 4, 2, 6, 8, 10)
+PACKED = 68
+RELAYED = 30
 
 
 def kernel(
     n_grp, n_dev, fields, swap_dev, swap_grp, neighbors_hbm, orient_hbm, out,
     neighbors, orient,
-    raw, moved, state0, state1, partial, result, faces0, faces1, ghosts0, ghosts1, chosen, walls_y, walls_z,
-    small_sem, load_sem, store_sem, move_send, move_recv, send_sem, recv_sem,
+    raw, moved, state0, state1, partial, packed, faces1, own1, far1, ghosts1, chosen, walls_y, walls_z,
+    short3, beside, relayed, passed, outer3, outer0, beyond,
+    small_sem, load_sem, send_sem, recv_sem, pass_send, pass_recv, first_send, first_recv,
 ):
     grp, dev = lax.axis_index("grp"), lax.axis_index("dev")
     rank = grp * n_dev + dev
-    pair_dev = dev + 1 - 2 * lax.rem(dev, 2)
-    pair_grp = grp + 1 - 2 * lax.rem(grp, 2)
+    odd, odd_grp = lax.rem(dev, 2), lax.rem(grp, 2)
+    even = odd == 0
+    even_grp = odd_grp == 0
+    pair_dev, pair_grp = dev + 1 - 2 * odd, grp + 1 - 2 * odd_grp
+    out_dev, out_grp = dev - 1 + 2 * odd, grp - 1 + 2 * odd_grp
+    relay = dev + 1 - odd
     has_below_dev, has_above_dev = dev > 0, dev < n_dev - 1
     has_below_grp, has_above_grp = grp > 0, grp < n_grp - 1
+    has_outer = jnp.where(even, has_below_dev, has_above_dev)
+    to_last = jnp.where(even, dev + 2, dev - 2)
+    from_last = jnp.where(even, dev - 2, dev + 2)
+    to_first = jnp.where(even_grp, grp + 2, grp - 2)
+    from_first = jnp.where(even_grp, grp - 2, grp + 2)
+    has_to_last = (to_last >= 0) & (to_last < n_dev)
+    has_from_last = (from_last >= 0) & (from_last < n_dev)
+    has_to_first = (to_first >= 0) & (to_first < n_grp)
+    has_from_first = (from_first >= 0) & (from_first < n_grp)
     sides = (
         (has_below_dev, {"dev": dev - 1}),
         (has_above_dev, {"dev": dev + 1}),
         (has_below_grp, {"grp": grp - 1}),
         (has_above_grp, {"grp": grp + 1}),
     )
+    above_relay = {"grp": grp + 1, "dev": relay}
+    below_relay = {"grp": grp - 1, "dev": relay}
+    pair_relay = {"grp": pair_grp, "dev": relay}
+    outer_pair = {"grp": pair_grp, "dev": out_dev}
+    is_odd = odd == 1
 
     barrier = pltpu.get_barrier_semaphore()
-    for there, target in sides:
+    sources = (
+        sides[0], sides[1],
+        (is_odd & has_below_grp, {"grp": grp - 1, "dev": dev}),
+        (is_odd & has_above_grp, {"grp": grp + 1, "dev": dev}),
+        (is_odd & has_below_grp, {"grp": grp - 1, "dev": dev - 1}),
+        (is_odd & has_above_grp, {"grp": grp + 1, "dev": dev - 1}),
+        (has_from_last, {"dev": from_last}),
+        (has_outer, outer_pair),
+        (has_from_first, {"grp": from_first}),
+    )
+    for there, target in sources:
 
         @pl.when(there)
         def _():
             pl.semaphore_signal(barrier, inc=1, device_id=target, device_id_type=MESH)
 
     smalls = [
-        pltpu.make_async_copy(source, into, small_sem.at[number])
-        for number, (source, into) in enumerate(
-            (
-                (neighbors_hbm, neighbors),
-                (orient_hbm, orient),
-            )
-        )
+        pltpu.make_async_copy(neighbors_hbm, neighbors, small_sem.at[0]),
+        pltpu.make_async_copy(orient_hbm, orient, small_sem.at[1]),
     ]
     loads = []
     for half in range(HALVES):
@@ -93,26 +138,7 @@
                     load_sem.at[half * SLOTS + slot],
                 )
             )
-    for copy in smalls + loads:
-        copy.start()
-    peers = [jnp.where(there, 1, 0) for there, _ in sides]
-    pl.semaphore_wait(barrier, peers[0] + peers[1] + peers[2] + peers[3])
-
-    moves = []
-    for slot, target in ((0, {"grp": pair_grp}), (SLOTS - 1, {"dev": pair_dev})):
-        for half in range(HALVES):
-            index = len(moves)
-            moves.append(
-                pltpu.make_async_remote_copy(
-                    src_ref=fields.at[slot, :, :, pl.ds(half * LANES, LANES)],
-                    dst_ref=moved.at[half, :, slot],
-                    send_sem=move_send.at[index],
-                    recv_sem=move_recv.at[index],
-                    device_id=target,
-                    device_id_type=MESH,
-                )
-            )
-    for copy in moves:
+    for copy in loads + smalls:
         copy.start()
 
     row = lax.broadcasted_iota(jnp.int32, (8, LANES), 0)
@@ -160,7 +186,7 @@
         (slot_of == SLOTS - 1) & (swap_dev[0] == 1)
     )
 
-    def pack_y(state, faces):
+    def pack_y(state, put):
         for side in range(2):
             for tile in range(TILES):
                 low, high = zero, zero
@@ -170,10 +196,10 @@
                     turned = roll(both, 16 * k)
                     low = jnp.where(column == k, turned, low)
                     high = jnp.where(column == (k + 7) % 8, turned, high)
-                faces[0, side, tile] = low
-                faces[1, side, tile] = roll(high, 16)
-
-    def pack_z(state, faces):
+                put(2, side, tile, low)
+                put(3, side, tile, roll(high, 16))
+
+    def pack_z(state, put):
         for half in range(HALVES):
             for tile in range(TILES):
                 low, high = zero, zero
@@ -181,10 +207,10 @@
                     turned = roll(state[x, half, tile], x)
                     low = jnp.where(z == x, turned, low)
                     high = jnp.where(z == (x + 15) % 16, turned, high)
-                faces[2, half, tile] = low
-                faces[3, half, tile] = roll(high, -15)
-
-    def exchange(state, faces, ghosts, first):
+                put(4, half, tile, low)
+                put(5, half, tile, roll(high, -15))
+
+    def exchange(state, faces, ghosts):
         plan = (
             (state.at[EDGE - 1], 0, 1),
             (state.at[0], 1, 0),
@@ -198,8 +224,8 @@
                 pltpu.make_async_remote_copy(
                     src_ref=source,
                     dst_ref=ghosts.at[into],
-                    send_sem=send_sem.at[first + into],
-                    recv_sem=recv_sem.at[first + into],
+                    send_sem=send_sem.at[into],
+                    recv_sem=recv_sem.at[into],
                     device_id=sides[side][1],
                     device_id_type=MESH,
                 ),
@@ -216,19 +242,12 @@
             def _():
                 copy.start()
 
-    def choose(state, faces, ghosts, copies):
-        own = (state.at[0], state.at[EDGE - 1], faces.at[0], faces.at[1], faces.at[2], faces.at[3])
-        for copy, _, comes in copies:
-
-            @pl.when(comes)
-            def _():
-                copy.wait_recv()
-
+    def choose(own, ghosts):
         def pick(face, part, tile):
             outer, local, source_row = picks[face]
-            near = jnp.take_along_axis(own[face ^ 1][part, tile], source_row, axis=0)
+            near = jnp.take_along_axis(own(face ^ 1, part, tile), source_row, axis=0)
             far = jnp.take_along_axis(ghosts[face, part, tile], source_row, axis=0)
-            return jnp.where(outer, own[face][part, tile], jnp.where(local, near, far))
+            return jnp.where(outer, own(face, part, tile), jnp.where(local, near, far))
 
         for part in range(2):
             for tile in range(TILES):
@@ -297,59 +316,231 @@
         for half in range(HALVES):
             for tile in range(TILES):
                 state0[x, half, tile] = read_rows(raw, half, tile, x)
-    for copy in moves:
-        copy.wait_recv()
+
+    def put_packed(face, part, tile, v):
+        packed[FACE_AT[face] + part * TILES + tile] = v
+
+    def layer(face, part, tile):
+        return packed[FACE_AT[face] + part * TILES + tile]
+
+    for part in range(2):
+        for tile in range(TILES):
+            put_packed(0, part, tile, state0[0, part, tile])
+            put_packed(1, part, tile, state0[EDGE - 1, part, tile])
+    pack_y(state0, put_packed)
+    pack_z(state0, put_packed)
+    flags = jnp.where(swapped_here, 1.0, zero)
+    for at in FLAGS_AT:
+        packed[at] = flags
+    for face in range(6):
+        for part in range(2):
+            tiles = [layer(face, part, tile) for tile in range(TILES)]
+            first, last = tiles[0], zero
+            for tile in range(TILES):
+                shift = (tile - (SLOTS - 1)) % 8
+                first = jnp.where(slot_of == tile, pltpu.roll(tiles[tile], tile, 0) if tile else tiles[0], first)
+                last = jnp.where(slot_of == tile, pltpu.roll(tiles[tile], shift, 0), last)
+            packed[FIRST_AT + SHORT_AT[face] + part] = first
+            packed[LAST_AT + SHORT_AT[face] + part] = last
+            if face >= 4:
+                packed[Z_BLOCK_AT[face - 4] + part] = last
+
+    count = jnp.int32(0)
+    for there in (
+        has_below_dev, has_above_dev, has_below_grp, has_above_grp, has_to_last, has_outer, has_to_first
+    ):
+        count = count + jnp.where(there, 1, 0)
+    pl.semaphore_wait(barrier, count)
+
+    always = rank >= 0
+    sends = []
+
+    def send(source, into, number, slot, there, target):
+        copy = pltpu.make_async_remote_copy(
+            src_ref=source,
+            dst_ref=into,
+            send_sem=first_send.at[number],
+            recv_sem=first_recv.at[slot],
+            device_id=target,
+            device_id_type=MESH,
+        )
+
+        @pl.when(there)
+        def _():
+            copy.start()
+
+        sends.append((copy, there))
+
+    def received(into, slot, there):
+        @pl.when(there)
+        def _():
+            pltpu.make_async_remote_copy(
+                src_ref=into,
+                dst_ref=into,
+                send_sem=first_send.at[0],
+                recv_sem=first_recv.at[slot],
+                device_id={"dev": pair_dev},
+                device_id_type=MESH,
+            ).wait_recv()
+
+    send(packed.at[pl.ds(26, 9)], relayed.at[odd, pl.ds(12, 9)], 0, 8 + 5 * odd, has_below_grp, below_relay)
+    send(packed.at[pl.ds(35, 9)], relayed.at[odd, pl.ds(21, 9)], 1, 9 + 5 * odd, has_above_grp, above_relay)
+    send(packed.at[pl.ds(FIRST_AT, 12)], relayed.at[odd, pl.ds(0, 12)], 2, 10 + 5 * odd, always, pair_relay)
+    send(packed.at[pl.ds(0, 13)], beside.at[0], 3, 0, has_below_dev, sides[0][1])
+    send(packed.at[pl.ds(13, 13)], beside.at[1], 4, 1, has_above_dev, sides[1][1])
+    send(packed.at[pl.ds(LAST_AT, 12)], short3, 5, 2, always, {"dev": pair_dev})
+    for half in range(HALVES):
+        lanes = pl.ds(half * LANES, LANES)
+        send(
+            fields.at[0, :, :, lanes], passed.at[odd, half], 6 + half, 11 + half + 5 * odd, always, pair_relay
+        )
+    send(
+        packed.at[pl.ds(LAST_AT + jnp.where(even, 4, 0), 4)], outer3, 8, 5, has_to_last, {"dev": to_last}
+    )
+    send(packed.at[pl.ds(FIRST_AT + jnp.where(even, 0, 4), 4)], outer0, 9, 6, has_outer, outer_pair)
+    send(
+        packed.at[pl.ds(FIRST_AT + jnp.where(even_grp, 10, 8), 2)], beyond, 10, 7, has_to_first, {"grp": to_first}
+    )
+    for half in range(HALVES):
+        lanes = pl.ds(half * LANES, LANES)
+        send(fields.at[SLOTS - 1, :, :, lanes], moved.at[half, :, SLOTS - 1], 11 + half, 3 + half, always, {"dev": pair_dev})
+
+    passes = [
+        pltpu.make_async_remote_copy(
+            src_ref=ref,
+            dst_ref=ref,
+            send_sem=pass_send.at[number],
+            recv_sem=pass_recv.at[number],
+            device_id={"dev": pair_dev},
+            device_id_type=MESH,
+        )
+        for number, ref in enumerate((relayed, passed.at[0]))
+    ]
+    for parity in range(2):
+        base = 8 + 5 * parity
+        received(relayed.at[parity, pl.ds(12, 9)], base, is_odd & has_above_grp)
+        received(relayed.at[parity, pl.ds(21, 9)], base + 1, is_odd & has_below_grp)
+        received(relayed.at[parity, pl.ds(0, 12)], base + 2, is_odd)
+
+    @pl.when(is_odd)
+    def _():
+        passes[0].start()
+
+    for half in range(HALVES):
+        received(passed.at[0, half], 11 + half, is_odd)
+
+    @pl.when(is_odd)
+    def _():
+        passes[1].start()
+
+    for half in range(HALVES):
+        received(passed.at[1, half], 16 + half, is_odd)
+
+    @pl.when(even)
+    def _():
+        for copy in passes:
+            copy.wait_recv()
+
+    for half in range(HALVES):
+        received(moved.at[half, :, SLOTS - 1], 3 + half, always)
+    received(beside.at[0], 0, has_above_dev)
+    received(beside.at[1], 1, has_below_dev)
+    received(short3, 2, always)
+    received(outer3, 5, has_from_last)
+    received(outer0, 6, has_outer)
+    received(beyond, 7, has_from_first)
+
     order = (0, EDGE - 1, *range(1, EDGE - 1))
     for x in order:
         for half in range(HALVES):
             for tile in range(TILES):
                 state0[x, half, tile] = jnp.where(
-                    swapped_here, read_rows(moved, half, tile, x), state0[x, half, tile]
+                    swapped_here, read_moved(moved, passed, odd, half, tile, x), state0[x, half, tile]
                 )
-
-    first = exchange(state0, faces0, ghosts0, 0)
-    start(first[:2])
-    pack_z(state0, faces0)
-    start(first[4:])
-    pack_y(state0, faces0)
-    start(first[2:4])
     for x in range(EDGE):
         prepare(state0, x)
-    choose(state0, faces0, ghosts0, first)
+
+    def spread(first, last, tile):
+        return jnp.where(
+            slot_of == 0, pltpu.roll(first, (8 - tile) % 8, 0) if tile else first, pltpu.roll(last, 3 - tile, 0)
+        )
+
+    is_first = slot_of == 0
+    for face in range(6):
+        at = SHORT_AT[face]
+        for part in range(2):
+            for tile in range(TILES):
+                swapped = spread(relayed[odd, at + part], short3[at + part], tile)
+                own1[face, part, tile] = jnp.where(swapped_here, swapped, layer(face, part, tile))
+    for face in range(4):
+        side = face % 2
+        there = face ^ 1
+        short = SHORT_AT[there] % 4
+        near = even if side == 1 else is_odd
+        landed = beside.at[1 - side]
+        begin = 6 * (face // 2)
+        flagged = landed[12] > 0.5
+        for part in range(2):
+            first = jnp.where(near, relayed[1 - odd, SHORT_AT[there] + part], outer0[short + part])
+            for tile in range(TILES):
+                mine = layer(there, part, tile)
+                apart = spread(first, outer3[short + part], tile)
+                swapped = jnp.where(is_first, apart, jnp.where(near, mine, apart))
+                far1[face, part, tile] = jnp.where(flagged, swapped, landed[begin + part * TILES + tile])
+    for face in (4, 5):
+        there = face ^ 1
+        begin = 12 if face == 5 else 21
+        near = even_grp if face == 5 else odd_grp == 1
+        flagged = relayed[odd, begin + 6] > 0.5
+        for part in range(2):
+            for tile in range(TILES):
+                apart = spread(beyond[part], relayed[1 - odd, begin + 7 + part], tile)
+                swapped = jnp.where(is_first & near, layer(there, part, tile), apart)
+                far1[face, part, tile] = jnp.where(
+                    flagged, swapped, relayed[odd, begin + part * TILES + tile]
+                )
+    choose(lambda face, part, tile: own1[face, part, tile], far1)
 
     for x in order:
         for half in range(HALVES):
             for tile in range(TILES):
                 state1[x, half, tile] = finish(x, half, tile)
-    second = exchange(state1, faces1, ghosts1, 6)
+
+    def put_faces(face, part, tile, v):
+        faces1[face - 2, part, tile] = v
+
+    second = exchange(state1, faces1, ghosts1)
     start(second[:2])
-    pack_z(state1, faces1)
+    pack_y(state1, put_faces)
+    start(second[2:4])
+    pack_z(state1, put_faces)
     start(second[4:])
-    pack_y(state1, faces1)
-    start(second[2:4])
     for x in range(EDGE):
         prepare(state1, x)
-    choose(state1, faces1, ghosts1, second)
-
-    stores = []
+    for copy, _, comes in second:
+
+        @pl.when(comes)
+        def _():
+            copy.wait_recv()
+
+    def own2(face, part, tile):
+        if face < 2:
+            return state1[(EDGE - 1) * face, part, tile]
+        return faces1[face - 2, part, tile]
+
+    choose(own2, ghosts1)
+
     for half in range(HALVES):
         for x in range(EDGE):
             for tile in range(TILES):
-                write_rows(result, half, tile, x, finish(x, half, tile))
-        for slot in range(SLOTS):
-            stores.append(
-                pltpu.make_async_copy(
-                    result.at[half, :, slot],
-                    out.at[slot, :, :, pl.ds(half * LANES, LANES)],
-                    store_sem.at[half * SLOTS + slot],
-                )
-            )
-            stores[-1].start()
-    for copy in stores:
-        copy.wait()
-    for copy in moves:
-        copy.wait_send()
-    for copy, there, _ in first + second:
+                write_rows(out, half, tile, x, finish(x, half, tile))
+
+    @pl.when(is_odd)
+    def _():
+        for copy in passes:
+            copy.wait_send()
+
+    for copy, there, *_ in sends + second:
 
         @pl.when(there)
         def _():
@@ -363,16 +554,18 @@
         block = (HALVES, NFIELD, SLOTS, EDGE, LANES)
         plane = (HALVES, TILES, 8, LANES)
         smalls = (neighbors, orient)
-        shapes = [block, block] + [(EDGE,) + plane] * 3 + [block]
-        shapes += [(4,) + plane, (4,) + plane, (6,) + plane, (6,) + plane] + [(2,) + plane] * 3
-        return pl.pallas_call(
+        cells = [(EDGE,) + plane] * 3
+        shapes = [block, block, *cells, (PACKED, 8, LANES), (4,) + plane, *[(6,) + plane] * 3, *[(2,) + plane] * 3]
+        shapes += [(12, 8, LANES), (2, 13, 8, LANES), (2, RELAYED, 8, LANES), (2, HALVES, NFIELD, EDGE, LANES)]
+        shapes += [(4, 8, LANES), (4, 8, LANES), (2, 8, LANES)]
+        new = pl.pallas_call(
             functools.partial(kernel, n_grp, n_dev),
-            out_shape=jax.ShapeDtypeStruct(fields.shape, fields.dtype),
+            out_shape=jax.ShapeDtypeStruct((SLOTS, NFIELD, 2, HALVES, 8, LANES), fields.dtype),
             in_specs=[pl.BlockSpec(memory_space=space) for space in (pl.ANY, pltpu.SMEM, pltpu.SMEM, pl.ANY, pl.ANY)],
-            out_specs=pl.BlockSpec(memory_space=pl.ANY),
+            out_specs=pl.BlockSpec(memory_space=pltpu.VMEM),
             scratch_shapes=[pltpu.SMEM(a.shape, a.dtype) for a in smalls]
             + [pltpu.VMEM(shape, jnp.float32) for shape in shapes]
-            + [pltpu.SemaphoreType.DMA((n,)) for n in (2, 8, 8, 4, 4, 12, 12)],
+            + [pltpu.SemaphoreType.DMA((n,)) for n in (2, 8, 6, 6, 2, 2, 13, 18)],
             compiler_params=pltpu.CompilerParams(
                 collective_id=0, has_side_effects=True, vmem_limit_bytes=16 * 2**20
             ),
@@ -380,6 +573,7 @@
         )(
             in_hbm(fields), swap_dev, swap_grp, *[in_hbm(a) for a in smalls]
         )
+        return new.transpose(0, 1, 2, 4, 3, 5).reshape(fields.shape)
 
     in_specs = (
         P(("grp", "dev"), None, None, None),

time: 28 us -> 27.9 us (level)
  no operation moved by 1% of the time
where the time goes in v3:
time: 27.9 us; the launch traced here: 27.7 us
  Pallas kernels  25.7 us (92%)
  between operations  1.3 us (5%)
  local copies, waits for them, and re-layouts  0.75 us (3%)
    pallas_call x1, Pallas kernels, body(): pl.pallas_call(functools.partial(kernel, n_grp, n_dev), out_shape=jax.Sha...  25.7 us
    unnamed x1, local copies, waits for them, and re-layouts  0.75 us

profile of v3, /device:TPU:1, one launch (start us, length us, event | category | flops | bytes accessed | tf_op | source)
XLA Modules:
  0.0 27.7 jit_solution(1308890136669144726)
XLA Ops:
  1.3 25.7 %phase_field_steps.1 = f32[4,6,2,2,8,128]{5,4,3,2,1,0:T(8,128)S(1)} custom-call(f32[4,6,16,256]{3,2,1,0:T(8,128)} %fields.1, s32[1]{0:T(128)S(6)} %copy.7.swap_dev, s32[1]{0:T(128)S(6)} %copy.8.swap_grp, s32[4,6]{1,0:T(4,128)} %neighbors_hbm.1, s32[4]{0:T(128)} %orient_hbm.1), custom_call_target="tpu_custom_call" | custom-call | tf_op jit(solution)/shard_map/phase_field_steps/pallas_call | solution.py:561
  27.0 0.7 %copy.9 = f32[4,6,16,256]{3,2,1,0:T(8,128)} copy(f32[4,6,16,256]{3,2,1,0:T(8,128)S(1)} %bitcast.3) | data formatting | bytes 786432

commit v4 on v3

--- a/solution.py
+++ b/solution.py
@@ -74,7 +74,7 @@
     neighbors, orient,
     raw, moved, state0, state1, partial, packed, faces1, own1, far1, ghosts1, chosen, walls_y, walls_z,
     short3, beside, relayed, passed, outer3, outer0, beyond,
-    small_sem, load_sem, send_sem, recv_sem, pass_send, pass_recv, first_send, first_recv,
+    small_sem, load_sem, send_sem, recv_sem, pass_send, pass_recv, first_send, first_recv, ready_sem,
 ):
     grp, dev = lax.axis_index("grp"), lax.axis_index("dev")
     rank = grp * n_dev + dev
@@ -109,7 +109,7 @@
 
     barrier = pltpu.get_barrier_semaphore()
     sources = (
-        sides[0], sides[1],
+        sides[0], (is_odd & has_above_dev, {"dev": dev + 1}),
         (is_odd & has_below_grp, {"grp": grp - 1, "dev": dev}),
         (is_odd & has_above_grp, {"grp": grp + 1, "dev": dev}),
         (is_odd & has_below_grp, {"grp": grp - 1, "dev": dev - 1}),
@@ -347,12 +347,17 @@
 
     count = jnp.int32(0)
     for there in (
-        has_below_dev, has_above_dev, has_below_grp, has_above_grp, has_to_last, has_outer, has_to_first
+        has_below_dev & even, has_above_dev, has_below_grp, has_above_grp, has_to_last, has_outer, has_to_first
     ):
         count = count + jnp.where(there, 1, 0)
     pl.semaphore_wait(barrier, count)
 
     always = rank >= 0
+
+    @pl.when(even)
+    def _():
+        pl.semaphore_signal(ready_sem, inc=1, device_id={"dev": pair_dev}, device_id_type=MESH)
+
     sends = []
 
     def send(source, into, number, slot, there, target):
@@ -386,14 +391,12 @@
     send(packed.at[pl.ds(26, 9)], relayed.at[odd, pl.ds(12, 9)], 0, 8 + 5 * odd, has_below_grp, below_relay)
     send(packed.at[pl.ds(35, 9)], relayed.at[odd, pl.ds(21, 9)], 1, 9 + 5 * odd, has_above_grp, above_relay)
     send(packed.at[pl.ds(FIRST_AT, 12)], relayed.at[odd, pl.ds(0, 12)], 2, 10 + 5 * odd, always, pair_relay)
-    send(packed.at[pl.ds(0, 13)], beside.at[0], 3, 0, has_below_dev, sides[0][1])
-    send(packed.at[pl.ds(13, 13)], beside.at[1], 4, 1, has_above_dev, sides[1][1])
-    send(packed.at[pl.ds(LAST_AT, 12)], short3, 5, 2, always, {"dev": pair_dev})
     for half in range(HALVES):
         lanes = pl.ds(half * LANES, LANES)
         send(
             fields.at[0, :, :, lanes], passed.at[odd, half], 6 + half, 11 + half + 5 * odd, always, pair_relay
         )
+    send(packed.at[pl.ds(13 * odd, 13)], beside.at[odd], 3, odd, has_outer, {"dev": out_dev})
     send(
         packed.at[pl.ds(LAST_AT + jnp.where(even, 4, 0), 4)], outer3, 8, 5, has_to_last, {"dev": to_last}
     )
@@ -401,6 +404,13 @@
     send(
         packed.at[pl.ds(FIRST_AT + jnp.where(even_grp, 10, 8), 2)], beyond, 10, 7, has_to_first, {"grp": to_first}
     )
+
+    @pl.when(is_odd)
+    def _():
+        pl.semaphore_wait(ready_sem, 1)
+
+    send(packed.at[pl.ds(13 * (1 - odd), 13)], beside.at[1 - odd], 4, 1 - odd, always, {"dev": pair_dev})
+    send(packed.at[pl.ds(LAST_AT, 12)], short3, 5, 2, always, {"dev": pair_dev})
     for half in range(HALVES):
         lanes = pl.ds(half * LANES, LANES)
         send(fields.at[SLOTS - 1, :, :, lanes], moved.at[half, :, SLOTS - 1], 11 + half, 3 + half, always, {"dev": pair_dev})
@@ -414,51 +424,73 @@
             device_id={"dev": pair_dev},
             device_id_type=MESH,
         )
-        for number, ref in enumerate((relayed, passed.at[0]))
+        for number, ref in enumerate(
+            (
+                relayed.at[:, pl.ds(12, 9)],
+                relayed.at[:, pl.ds(21, 9)],
+                relayed.at[:, pl.ds(0, 12)],
+                passed.at[0],
+            )
+        )
     ]
-    for parity in range(2):
-        base = 8 + 5 * parity
-        received(relayed.at[parity, pl.ds(12, 9)], base, is_odd & has_above_grp)
-        received(relayed.at[parity, pl.ds(21, 9)], base + 1, is_odd & has_below_grp)
-        received(relayed.at[parity, pl.ds(0, 12)], base + 2, is_odd)
-
-    @pl.when(is_odd)
-    def _():
-        passes[0].start()
-
-    for half in range(HALVES):
-        received(passed.at[0, half], 11 + half, is_odd)
-
-    @pl.when(is_odd)
-    def _():
-        passes[1].start()
-
+
+    def pass_on(number, there):
+        @pl.when(there)
+        def _():
+            passes[number].start()
+
+    def relay_layers(number, there):
+        for parity in range(2):
+            received(relayed.at[parity, pl.ds(12 + 9 * number, 9)], 8 + number + 5 * parity, there)
+        pass_on(number, there)
+
+    def relay_first(there):
+        for parity in range(2):
+            received(relayed.at[parity, pl.ds(0, 12)], 10 + 5 * parity, there)
+        pass_on(2, there)
+
+    def relay_block(there):
+        for half in range(HALVES):
+            received(passed.at[0, half], 11 + half, there)
+        pass_on(3, there)
+
+    relay_layers(0, is_odd & has_above_grp)
+    relay_first(is_odd & even_grp)
+    relay_block(is_odd & even_grp)
     for half in range(HALVES):
         received(passed.at[1, half], 16 + half, is_odd)
 
     @pl.when(even)
     def _():
-        for copy in passes:
-            copy.wait_recv()
+        passes[3].wait_recv()
 
     for half in range(HALVES):
         received(moved.at[half, :, SLOTS - 1], 3 + half, always)
+
+    order = (0, EDGE - 1, *range(1, EDGE - 1))
+    for x in order:
+        for half in range(HALVES):
+            for tile in range(TILES):
+                state0[x, half, tile] = jnp.where(
+                    swapped_here, read_moved(moved, passed, odd, half, tile, x), state0[x, half, tile]
+                )
+    for x in range(EDGE):
+        prepare(state0, x)
+
+    relay_layers(1, is_odd & has_below_grp)
+    relay_first(is_odd & (odd_grp == 1))
+    for number, there in ((0, even & has_above_grp), (1, even & has_below_grp), (2, even)):
+
+        @pl.when(there)
+        def _():
+            passes[number].wait_recv()
+
     received(beside.at[0], 0, has_above_dev)
     received(beside.at[1], 1, has_below_dev)
     received(short3, 2, always)
     received(outer3, 5, has_from_last)
     received(outer0, 6, has_outer)
     received(beyond, 7, has_from_first)
-
-    order = (0, EDGE - 1, *range(1, EDGE - 1))
-    for x in order:
-        for half in range(HALVES):
-            for tile in range(TILES):
-                state0[x, half, tile] = jnp.where(
-                    swapped_here, read_moved(moved, passed, odd, half, tile, x), state0[x, half, tile]
-                )
-    for x in range(EDGE):
-        prepare(state0, x)
 
     def spread(first, last, tile):
         return jnp.where(
@@ -511,10 +543,11 @@
 
     second = exchange(state1, faces1, ghosts1)
     start(second[:2])
+    pack_z(state1, put_faces)
+    start(second[4:])
     pack_y(state1, put_faces)
     start(second[2:4])
-    pack_z(state1, put_faces)
-    start(second[4:])
+    relay_block(is_odd & (odd_grp == 1))
     for x in range(EDGE):
         prepare(state1, x)
     for copy, _, comes in second:
@@ -535,10 +568,13 @@
             for tile in range(TILES):
                 write_rows(out, half, tile, x, finish(x, half, tile))
 
-    @pl.when(is_odd)
-    def _():
-        for copy in passes:
-            copy.wait_send()
+    for number, there in (
+        (0, is_odd & has_above_grp), (1, is_odd & has_below_grp), (2, is_odd), (3, is_odd)
+    ):
+
+        @pl.when(there)
+        def _():
+            passes[number].wait_send()
 
     for copy, there, *_ in sends + second:
 
@@ -565,7 +601,8 @@
             out_specs=pl.BlockSpec(memory_space=pltpu.VMEM),
             scratch_shapes=[pltpu.SMEM(a.shape, a.dtype) for a in smalls]
             + [pltpu.VMEM(shape, jnp.float32) for shape in shapes]
-            + [pltpu.SemaphoreType.DMA((n,)) for n in (2, 8, 6, 6, 2, 2, 13, 18)],
+            + [pltpu.SemaphoreType.DMA((n,)) for n in (2, 8, 6, 6, 4, 4, 13, 18)]
+            + [pltpu.SemaphoreType.REGULAR],
             compiler_params=pltpu.CompilerParams(
                 collective_id=0, has_side_effects=True, vmem_limit_bytes=16 * 2**20
             ),

time: 27.9 us -> 25.3 us (0.907)
  Pallas kernels: 25.7 us -> 23.1 us
    pallas_call x1, Pallas kernels: 25.7 us -> 23.1 us  [body(): pl.pallas_call(functools.partial(kernel, n_grp, n_dev), out_shape=jax.Sha...]
where the time goes in v4:
time: 25.3 us; the launch traced here: 25.1 us
  Pallas kernels  23.1 us (91%)
  between operations  1.3 us (5%)
  local copies, waits for them, and re-layouts  0.75 us (3%)
    pallas_call x1, Pallas kernels, body(): pl.pallas_call(functools.partial(kernel, n_grp, n_dev), out_shape=jax.Sha...  23.1 us
    unnamed x1, local copies, waits for them, and re-layouts  0.75 us

profile of v4, /device:TPU:1, one launch (start us, length us, event | category | flops | bytes accessed | tf_op | source)
XLA Modules:
  0.0 25.1 jit_solution(18148751325191215420)
XLA Ops:
  1.3 23.1 %phase_field_steps.1 = f32[4,6,2,2,8,128]{5,4,3,2,1,0:T(8,128)S(1)} custom-call(f32[4,6,16,256]{3,2,1,0:T(8,128)} %fields.1, s32[1]{0:T(128)S(6)} %copy.7.swap_dev, s32[1]{0:T(128)S(6)} %copy.8.swap_grp, s32[4,6]{1,0:T(4,128)} %neighbors_hbm.1, s32[4]{0:T(128)} %orient_hbm.1), custom_call_target="tpu_custom_call" | custom-call | tf_op jit(solution)/shard_map/phase_field_steps/pallas_call | solution.py:597
  24.4 0.7 %copy.9 = f32[4,6,16,256]{3,2,1,0:T(8,128)} copy(f32[4,6,16,256]{3,2,1,0:T(8,128)S(1)} %bitcast.3) | data formatting | bytes 786432

commit v5 on v4

--- a/solution.py
+++ b/solution.py
@@ -72,7 +72,7 @@
 def kernel(
     n_grp, n_dev, fields, swap_dev, swap_grp, neighbors_hbm, orient_hbm, out,
     neighbors, orient,
-    raw, moved, state0, state1, partial, packed, faces1, own1, far1, ghosts1, chosen, walls_y, walls_z,
+    raw, moved, state0, state1, partial, packed, faces1, own1, far1, ghosts1, picked, chosen, walls_y, walls_z,
     short3, beside, relayed, passed, outer3, outer0, beyond,
     small_sem, load_sem, send_sem, recv_sem, pass_send, pass_recv, first_send, first_recv, ready_sem,
 ):
@@ -242,7 +242,7 @@
             def _():
                 copy.start()
 
-    def choose(own, ghosts):
+    def choose(own, ghosts, along="xyz"):
         def pick(face, part, tile):
             outer, local, source_row = picks[face]
             near = jnp.take_along_axis(own(face ^ 1, part, tile), source_row, axis=0)
@@ -251,14 +251,20 @@
 
         for part in range(2):
             for tile in range(TILES):
-                chosen[0, part, tile] = pick(0, part, tile)
-                chosen[1, part, tile] = pick(1, part, tile)
-                below, above = roll(pick(2, part, tile), 16), pick(3, part, tile)
-                walls_y[0, part, tile] = jnp.where(column % 2 == 0, above, below)
-                walls_y[1, part, tile] = jnp.where(column % 2 == 1, above, below)
-                below, above = roll(pick(4, part, tile), -15), pick(5, part, tile)
-                walls_z[0, part, tile] = jnp.where(z % 2 == 0, above, below)
-                walls_z[1, part, tile] = jnp.where(z % 2 == 1, above, below)
+                if along != "z":
+                    chosen[0, part, tile] = pick(0, part, tile)
+                    chosen[1, part, tile] = pick(1, part, tile)
+                    below, above = pick(2, part, tile), pick(3, part, tile)
+                    picked[0, part, tile], picked[1, part, tile] = below, above
+                    below = roll(below, 16)
+                    walls_y[0, part, tile] = jnp.where(column % 2 == 0, above, below)
+                    walls_y[1, part, tile] = jnp.where(column % 2 == 1, above, below)
+                if along != "xy":
+                    below, above = pick(4, part, tile), pick(5, part, tile)
+                    picked[2, part, tile], picked[3, part, tile] = below, above
+                    below = roll(below, -15)
+                    walls_z[0, part, tile] = jnp.where(z % 2 == 0, above, below)
+                    walls_z[1, part, tile] = jnp.where(z % 2 == 1, above, below)
 
     def prepare(state, x):
         v = [[state[x, half, tile] for tile in range(TILES)] for half in range(HALVES)]
@@ -300,9 +306,7 @@
             )
             partial[x, half, 2] = linear[half][2]
 
-    def finish(x, half, tile):
-        v = partial[x, half, tile]
-        v = v + scales_z[tile] * roll(walls_z[x % 2, half, tile], 15 - x)
+    def finish_xy(v, x, half, tile):
         v = v + scales_y[half][tile] * roll(walls_y[x % 2, x // 8, tile], 16 * (7 - x % 8))
         if x == 0:
             v = v + scales_x[tile] * chosen[0, half, tile]
@@ -310,6 +314,9 @@
             v = v + scales_x[tile] * chosen[1, half, tile]
         return v
 
+    def finish_z(v, x, half, tile):
+        return v + scales_z[tile] * roll(walls_z[x % 2, half, tile], 15 - x)
+
     for copy in loads:
         copy.wait()
     for x in range(EDGE):
@@ -323,16 +330,7 @@
     def layer(face, part, tile):
         return packed[FACE_AT[face] + part * TILES + tile]
 
-    for part in range(2):
-        for tile in range(TILES):
-            put_packed(0, part, tile, state0[0, part, tile])
-            put_packed(1, part, tile, state0[EDGE - 1, part, tile])
-    pack_y(state0, put_packed)
-    pack_z(state0, put_packed)
-    flags = jnp.where(swapped_here, 1.0, zero)
-    for at in FLAGS_AT:
-        packed[at] = flags
-    for face in range(6):
+    def shorten(face):
         for part in range(2):
             tiles = [layer(face, part, tile) for tile in range(TILES)]
             first, last = tiles[0], zero
@@ -344,6 +342,13 @@
             packed[LAST_AT + SHORT_AT[face] + part] = last
             if face >= 4:
                 packed[Z_BLOCK_AT[face - 4] + part] = last
+
+    flags = jnp.where(swapped_here, 1.0, zero)
+    for at in FLAGS_AT:
+        packed[at] = flags
+    pack_z(state0, put_packed)
+    shorten(4)
+    shorten(5)
 
     count = jnp.int32(0)
     for there in (
@@ -390,12 +395,15 @@
 
     send(packed.at[pl.ds(26, 9)], relayed.at[odd, pl.ds(12, 9)], 0, 8 + 5 * odd, has_below_grp, below_relay)
     send(packed.at[pl.ds(35, 9)], relayed.at[odd, pl.ds(21, 9)], 1, 9 + 5 * odd, has_above_grp, above_relay)
+
+    for part in range(2):
+        for tile in range(TILES):
+            put_packed(0, part, tile, state0[0, part, tile])
+            put_packed(1, part, tile, state0[EDGE - 1, part, tile])
+    pack_y(state0, put_packed)
+    for face in range(4):
+        shorten(face)
     send(packed.at[pl.ds(FIRST_AT, 12)], relayed.at[odd, pl.ds(0, 12)], 2, 10 + 5 * odd, always, pair_relay)
-    for half in range(HALVES):
-        lanes = pl.ds(half * LANES, LANES)
-        send(
-            fields.at[0, :, :, lanes], passed.at[odd, half], 6 + half, 11 + half + 5 * odd, always, pair_relay
-        )
     send(packed.at[pl.ds(13 * odd, 13)], beside.at[odd], 3, odd, has_outer, {"dev": out_dev})
     send(
         packed.at[pl.ds(LAST_AT + jnp.where(even, 4, 0), 4)], outer3, 8, 5, has_to_last, {"dev": to_last}
@@ -404,6 +412,12 @@
     send(
         packed.at[pl.ds(FIRST_AT + jnp.where(even_grp, 10, 8), 2)], beyond, 10, 7, has_to_first, {"grp": to_first}
     )
+
+    for half in range(HALVES):
+        lanes = pl.ds(half * LANES, LANES)
+        send(
+            fields.at[0, :, :, lanes], passed.at[odd, half], 6 + half, 11 + half + 5 * odd, always, pair_relay
+        )
 
     @pl.when(is_odd)
     def _():
@@ -445,8 +459,7 @@
         pass_on(number, there)
 
     def relay_first(there):
-        for parity in range(2):
-            received(relayed.at[parity, pl.ds(0, 12)], 10 + 5 * parity, there)
+        received(relayed.at[0, pl.ds(0, 12)], 10, there)
         pass_on(2, there)
 
     def relay_block(there):
@@ -455,6 +468,7 @@
         pass_on(3, there)
 
     relay_layers(0, is_odd & has_above_grp)
+    received(relayed.at[1, pl.ds(0, 12)], 15, is_odd)
     relay_first(is_odd & even_grp)
     relay_block(is_odd & even_grp)
     for half in range(HALVES):
@@ -477,33 +491,45 @@
     for x in range(EDGE):
         prepare(state0, x)
 
-    relay_layers(1, is_odd & has_below_grp)
-    relay_first(is_odd & (odd_grp == 1))
-    for number, there in ((0, even & has_above_grp), (1, even & has_below_grp), (2, even)):
-
-        @pl.when(there)
-        def _():
-            passes[number].wait_recv()
-
-    received(beside.at[0], 0, has_above_dev)
-    received(beside.at[1], 1, has_below_dev)
-    received(short3, 2, always)
-    received(outer3, 5, has_from_last)
-    received(outer0, 6, has_outer)
-    received(beyond, 7, has_from_first)
-
     def spread(first, last, tile):
         return jnp.where(
             slot_of == 0, pltpu.roll(first, (8 - tile) % 8, 0) if tile else first, pltpu.roll(last, 3 - tile, 0)
         )
 
-    is_first = slot_of == 0
+    def put_faces(face, part, tile, v):
+        faces1[face - 2, part, tile] = v
+
+    pack_z(partial, put_faces)
+    pack_y(partial, put_faces)
+
+    received(short3, 2, always)
+
+    @pl.when(even)
+    def _():
+        passes[2].wait_recv()
+
     for face in range(6):
         at = SHORT_AT[face]
         for part in range(2):
             for tile in range(TILES):
                 swapped = spread(relayed[odd, at + part], short3[at + part], tile)
                 own1[face, part, tile] = jnp.where(swapped_here, swapped, layer(face, part, tile))
+
+    relay_layers(1, is_odd & has_below_grp)
+    relay_first(is_odd & (odd_grp == 1))
+    for number, there in ((0, even & has_above_grp), (1, even & has_below_grp)):
+
+        @pl.when(there)
+        def _():
+            passes[number].wait_recv()
+
+    received(beside.at[0], 0, has_above_dev)
+    received(beside.at[1], 1, has_below_dev)
+    received(outer3, 5, has_from_last)
+    received(outer0, 6, has_outer)
+    received(beyond, 7, has_from_first)
+
+    is_first = slot_of == 0
     for face in range(4):
         side = face % 2
         there = face ^ 1
@@ -533,40 +559,80 @@
                 )
     choose(lambda face, part, tile: own1[face, part, tile], far1)
 
-    for x in order:
+    all_x, all_y, all_z = (scale_x, scale_x, scale_c), (scale_y, scale_y, scale_c), (scale_z, scale_z, scale_c)
+
+    def lanes_of(v, index):
+        return jnp.take_along_axis(v, index, axis=1)
+
+    def z_layers(half, tile):
+        scale, wall = all_x[tile], all_y[tile]
+        for side in range(2):
+            at = 15 * side
+            index = 16 * (lane & 7) + at
+            edge = jnp.where(
+                (lane & 8) == 0,
+                lanes_of(picked[half, 0, tile], index),
+                lanes_of(picked[half, 1, tile], index),
+            )
+            v = faces1[2 + side, half, tile] + all_z[tile] * picked[2 + side, half, tile]
+            v = v + jnp.where(high_y if half else low_y, wall * edge, zero)
+            v = v + jnp.where(z == 0, scale * roll(chosen[0, half, tile], -at), zero)
+            v = v + jnp.where(z == EDGE - 1, scale * roll(chosen[1, half, tile], 15 - at), zero)
+            faces1[2 + side, half, tile] = v
+
+    def y_layers(part, tile):
+        scale, wall = all_x[tile], all_z[tile]
+        for side in range(2):
+            index = 112 * side + 8 * part + column
+            v = faces1[side, part, tile] + all_y[tile] * picked[side, part, tile]
+            v = v + jnp.where(z == 0, wall * lanes_of(picked[2, side, tile], index), zero)
+            v = v + jnp.where(z == EDGE - 1, wall * lanes_of(picked[3, side, tile], index), zero)
+            plane = roll(chosen[part, side, tile], 112 * part - 112 * side)
+            v = v + jnp.where(high_y if part else low_y, scale * plane, zero)
+            faces1[side, part, tile] = v
+
+    second = exchange(state1, faces1, ghosts1)
+    def advance_at(x):
         for half in range(HALVES):
             for tile in range(TILES):
-                state1[x, half, tile] = finish(x, half, tile)
-
-    def put_faces(face, part, tile, v):
-        faces1[face - 2, part, tile] = v
-
-    second = exchange(state1, faces1, ghosts1)
-    start(second[:2])
-    pack_z(state1, put_faces)
+                v = finish_xy(partial[x, half, tile], x, half, tile)
+                state1[x, half, tile] = finish_z(v, x, half, tile)
+
+    for x in order[:2]:
+        advance_at(x)
+    for part in range(2):
+        for tile in range(TILES):
+            y_layers(part, tile)
+    start(second[:4])
+    for part in range(2):
+        for tile in range(TILES):
+            z_layers(part, tile)
     start(second[4:])
-    pack_y(state1, put_faces)
-    start(second[2:4])
+    for x in order[2:]:
+        advance_at(x)
     relay_block(is_odd & (odd_grp == 1))
     for x in range(EDGE):
         prepare(state1, x)
-    for copy, _, comes in second:
-
-        @pl.when(comes)
-        def _():
-            copy.wait_recv()
+    def wait(copies):
+        for copy, _, comes in copies:
+
+            @pl.when(comes)
+            def _():
+                copy.wait_recv()
 
     def own2(face, part, tile):
         if face < 2:
             return state1[(EDGE - 1) * face, part, tile]
         return faces1[face - 2, part, tile]
 
+    wait(second)
     choose(own2, ghosts1)
 
     for half in range(HALVES):
         for x in range(EDGE):
             for tile in range(TILES):
-                write_rows(out, half, tile, x, finish(x, half, tile))
+                v = finish_xy(partial[x, half, tile], x, half, tile)
+                write_rows(out, half, tile, x, finish_z(v, x, half, tile))
 
     for number, there in (
         (0, is_odd & has_above_grp), (1, is_odd & has_below_grp), (2, is_odd), (3, is_odd)
@@ -591,7 +657,7 @@
         plane = (HALVES, TILES, 8, LANES)
         smalls = (neighbors, orient)
         cells = [(EDGE,) + plane] * 3
-        shapes = [block, block, *cells, (PACKED, 8, LANES), (4,) + plane, *[(6,) + plane] * 3, *[(2,) + plane] * 3]
+        shapes = [block, block, *cells, (PACKED, 8, LANES), (4,) + plane, *[(6,) + plane] * 3, (4,) + plane, *[(2,) + plane] * 3]
         shapes += [(12, 8, LANES), (2, 13, 8, LANES), (2, RELAYED, 8, LANES), (2, HALVES, NFIELD, EDGE, LANES)]
         shapes += [(4, 8, LANES), (4, 8, LANES), (2, 8, LANES)]
         new = pl.pallas_call(

time: 25.3 us -> 25 us (0.988)
  Pallas kernels: 23.1 us -> 22.8 us
    pallas_call x1, Pallas kernels: 23.1 us -> 22.8 us  [body(): pl.pallas_call(functools.partial(kernel, n_grp, n_dev), out_shape=jax.Sha...]
where the time goes in v5:
time: 25 us; the launch traced here: 24.8 us
  Pallas kernels  22.8 us (91%)
  between operations  1.3 us (5%)
  local copies, waits for them, and re-layouts  0.75 us (3%)
    pallas_call x1, Pallas kernels, body(): pl.pallas_call(functools.partial(kernel, n_grp, n_dev), out_shape=jax.Sha...  22.8 us
    unnamed x1, local copies, waits for them, and re-layouts  0.75 us

profile of v5, /device:TPU:1, one launch (start us, length us, event | category | flops | bytes accessed | tf_op | source)
XLA Modules:
  0.0 24.8 jit_solution(12215868341102526156)
XLA Ops:
  1.3 22.8 %phase_field_steps.1 = f32[4,6,2,2,8,128]{5,4,3,2,1,0:T(8,128)S(1)} custom-call(f32[4,6,16,256]{3,2,1,0:T(8,128)} %fields.1, s32[1]{0:T(128)S(6)} %copy.7.swap_dev, s32[1]{0:T(128)S(6)} %copy.8.swap_grp, s32[4,6]{1,0:T(4,128)} %neighbors_hbm.1, s32[4]{0:T(128)} %orient_hbm.1), custom_call_target="tpu_custom_call" | custom-call | tf_op jit(solution)/shard_map/phase_field_steps/pallas_call | solution.py:663
  24.1 0.7 %copy.9 = f32[4,6,16,256]{3,2,1,0:T(8,128)} copy(f32[4,6,16,256]{3,2,1,0:T(8,128)S(1)} %bitcast.3) | data formatting | bytes 786432

commit v6 on v5

--- a/solution.py
+++ b/solution.py
@@ -346,6 +346,13 @@
     flags = jnp.where(swapped_here, 1.0, zero)
     for at in FLAGS_AT:
         packed[at] = flags
+    for part in range(2):
+        for tile in range(TILES):
+            put_packed(0, part, tile, state0[0, part, tile])
+            put_packed(1, part, tile, state0[EDGE - 1, part, tile])
+    pack_y(state0, put_packed)
+    for face in range(4):
+        shorten(face)
     pack_z(state0, put_packed)
     shorten(4)
     shorten(5)
@@ -393,22 +400,15 @@
                 device_id_type=MESH,
             ).wait_recv()
 
-    send(packed.at[pl.ds(26, 9)], relayed.at[odd, pl.ds(12, 9)], 0, 8 + 5 * odd, has_below_grp, below_relay)
-    send(packed.at[pl.ds(35, 9)], relayed.at[odd, pl.ds(21, 9)], 1, 9 + 5 * odd, has_above_grp, above_relay)
-
-    for part in range(2):
-        for tile in range(TILES):
-            put_packed(0, part, tile, state0[0, part, tile])
-            put_packed(1, part, tile, state0[EDGE - 1, part, tile])
-    pack_y(state0, put_packed)
-    for face in range(4):
-        shorten(face)
-    send(packed.at[pl.ds(FIRST_AT, 12)], relayed.at[odd, pl.ds(0, 12)], 2, 10 + 5 * odd, always, pair_relay)
-    send(packed.at[pl.ds(13 * odd, 13)], beside.at[odd], 3, odd, has_outer, {"dev": out_dev})
+
     send(
         packed.at[pl.ds(LAST_AT + jnp.where(even, 4, 0), 4)], outer3, 8, 5, has_to_last, {"dev": to_last}
     )
     send(packed.at[pl.ds(FIRST_AT + jnp.where(even, 0, 4), 4)], outer0, 9, 6, has_outer, outer_pair)
+    send(packed.at[pl.ds(26, 9)], relayed.at[odd, pl.ds(12, 9)], 0, 8 + 5 * odd, has_below_grp, below_relay)
+    send(packed.at[pl.ds(35, 9)], relayed.at[odd, pl.ds(21, 9)], 1, 9 + 5 * odd, has_above_grp, above_relay)
+    send(packed.at[pl.ds(FIRST_AT, 12)], relayed.at[odd, pl.ds(0, 12)], 2, 10 + 5 * odd, always, pair_relay)
+    send(packed.at[pl.ds(13 * odd, 13)], beside.at[odd], 3, odd, has_outer, {"dev": out_dev})
     send(
         packed.at[pl.ds(FIRST_AT + jnp.where(even_grp, 10, 8), 2)], beyond, 10, 7, has_to_first, {"grp": to_first}
     )

time: 25 us -> 25 us (level)
  no operation moved by 1% of the time
where the time goes in v6:
time: 25 us; the launch traced here: 24.8 us
  Pallas kernels  22.7 us (91%)
  between operations  1.3 us (5%)
  local copies, waits for them, and re-layouts  0.75 us (3%)
    pallas_call x1, Pallas kernels, body(): pl.pallas_call(functools.partial(kernel, n_grp, n_dev), out_shape=jax.Sha...  22.7 us
    unnamed x1, local copies, waits for them, and re-layouts  0.75 us

profile of v6, /device:TPU:1, one launch (start us, length us, event | category | flops | bytes accessed | tf_op | source)
XLA Modules:
  0.0 24.8 jit_solution(11654627228489242864)
XLA Ops:
  1.3 22.7 %phase_field_steps.1 = f32[4,6,2,2,8,128]{5,4,3,2,1,0:T(8,128)S(1)} custom-call(f32[4,6,16,256]{3,2,1,0:T(8,128)} %fields.1, s32[1]{0:T(128)S(6)} %copy.7.swap_dev, s32[1]{0:T(128)S(6)} %copy.8.swap_grp, s32[4,6]{1,0:T(4,128)} %neighbors_hbm.1, s32[4]{0:T(128)} %orient_hbm.1), custom_call_target="tpu_custom_call" | custom-call | tf_op jit(solution)/shard_map/phase_field_steps/pallas_call | solution.py:663
  24.0 0.7 %copy.9 = f32[4,6,16,256]{3,2,1,0:T(8,128)} copy(f32[4,6,16,256]{3,2,1,0:T(8,128)S(1)} %bitcast.3) | data formatting | bytes 786432

commit v7 on v6

--- a/solution.py
+++ b/solution.py
@@ -625,15 +625,6 @@
             return state1[(EDGE - 1) * face, part, tile]
         return faces1[face - 2, part, tile]
 
-    wait(second)
-    choose(own2, ghosts1)
-
-    for half in range(HALVES):
-        for x in range(EDGE):
-            for tile in range(TILES):
-                v = finish_xy(partial[x, half, tile], x, half, tile)
-                write_rows(out, half, tile, x, finish_z(v, x, half, tile))
-
     for number, there in (
         (0, is_odd & has_above_grp), (1, is_odd & has_below_grp), (2, is_odd), (3, is_odd)
     ):
@@ -642,7 +633,22 @@
         def _():
             passes[number].wait_send()
 
-    for copy, there, *_ in sends + second:
+    for copy, there in sends:
+
+        @pl.when(there)
+        def _():
+            copy.wait_send()
+
+    wait(second)
+    choose(own2, ghosts1)
+
+    for half in range(HALVES):
+        for x in range(EDGE):
+            for tile in range(TILES):
+                v = finish_xy(partial[x, half, tile], x, half, tile)
+                write_rows(out, half, tile, x, finish_z(v, x, half, tile))
+
+    for copy, there, _ in second:
 
         @pl.when(there)
         def _():

time: 25 us -> 25 us (level)
  no operation moved by 1% of the time
where the time goes in v7:
time: 25 us; the launch traced here: 24.7 us
  Pallas kernels  22.7 us (91%)
  between operations  1.3 us (5%)
  local copies, waits for them, and re-layouts  0.75 us (3%)
    pallas_call x1, Pallas kernels, body(): pl.pallas_call(functools.partial(kernel, n_grp, n_dev), out_shape=jax.Sha...  22.7 us
    unnamed x1, local copies, waits for them, and re-layouts  0.75 us

profile of v7, /device:TPU:1, one launch (start us, length us, event | category | flops | bytes accessed | tf_op | source)
XLA Modules:
  0.0 24.7 jit_solution(4332607390926222862)
XLA Ops:
  1.3 22.7 %phase_field_steps.1 = f32[4,6,2,2,8,128]{5,4,3,2,1,0:T(8,128)S(1)} custom-call(f32[4,6,16,256]{3,2,1,0:T(8,128)} %fields.1, s32[1]{0:T(128)S(6)} %copy.7.swap_dev, s32[1]{0:T(128)S(6)} %copy.8.swap_grp, s32[4,6]{1,0:T(4,128)} %neighbors_hbm.1, s32[4]{0:T(128)} %orient_hbm.1), custom_call_target="tpu_custom_call" | custom-call | tf_op jit(solution)/shard_map/phase_field_steps/pallas_call | solution.py:669
  24.0 0.7 %copy.9 = f32[4,6,16,256]{3,2,1,0:T(8,128)} copy(f32[4,6,16,256]{3,2,1,0:T(8,128)S(1)} %bitcast.3) | data formatting | bytes 786432
